TPU v7x, 256 devices: a whole 4x4x8 slice. The times are simulated.
256 devices in a mesh: section: 8 (over z_lo, x), dp: 32 (over z_hi, y, core).
Axes of the slice: x: 4, y: 4, z: 8 (z_hi: 4, z_lo: 2; z = z_hi * 2 + z_lo), core: 2. Of those that a mesh axis runs over, the one named last changes fastest.
Arguments:
- incoming: bfloat16 [8, 4, 4096, 256], P('section', None, 'dp'), may hold values from -6 to 6
- feed: bfloat16 [4, 4, 4096, 256], P(None, None, 'dp'), may hold values from -6 to 6
- plan: int32 [1, 32], P(None, 'dp'), may hold values from 0 to 3, as said below
- weights: bfloat16 [8, 2, 27, 256, 256], P('section'), may hold values from -0.078125 to 0.078125
- momentum: float32 [8, 2, 27, 256, 256], P('section', None, None, 'dp'), may hold values from -6 to 6
Outputs:
- upstream: bfloat16 [2, 8, 4, 4096, 256], P(None, 'section', None, 'dp')
- new_momentum: float32 [8, 2, 27, 256, 256], P('section', None, None, 'dp')
Inputs may be any that keep to these rules, and one draw needn't show every extreme that they name: `plan`: every micro-batch of the pool is taken by some tile in some tick.
All inputs are finite; a program needn't handle non-finite values.
Results may differ from a plain program's by a relative error of at most 0.014.
Values may be sent and summed in bfloat16 or wider, within the bound.
No kernel may reach another device: no remote copies, remote signals or barrier semaphores. Data moves between devices by JAX's collectives and lax.ppermute only.
A program may use at most 128 MiB of HBM per device.

v0:
```python
import jax
import jax.numpy as jnp
from jax import lax
from jax.sharding import PartitionSpec as P

TD = 2
TH = 8
TW = 8
TICKS = 2


def shifted(array, axis, by):
    size = lax.axis_size(axis)
    pairs = [(i, i + by) for i in range(size) if 0 <= i + by < size]
    return lax.ppermute(array, axis, pairs)


def make_patches(act, sign):
    channels = act.shape[-1]
    volume = act.reshape(TD, TH, TW, channels)
    padded = jnp.pad(volume, ((1, 1), (1, 1), (1, 1), (0, 0)))
    pieces = []
    for depth in (-1, 0, 1):
        for height in (-1, 0, 1):
            for width in (-1, 0, 1):
                start_d = 1 + sign * depth
                start_h = 1 + sign * height
                start_w = 1 + sign * width
                cut = padded[start_d : start_d + TD, start_h : start_h + TH, start_w : start_w + TW]
                pieces.append(cut.reshape(-1, channels))
    return jnp.stack(pieces, axis=1)


def silu_grad(value):
    sig = jax.nn.sigmoid(value)
    return sig * (1.0 + value * (1.0 - sig))


def half_g(inputs, weight_g):
    y_one = inputs[0]
    y_two = inputs[1]
    dy_one = inputs[2]
    dy_two = inputs[3]
    y_one_f = y_one.astype(jnp.float32)
    act_one = jax.nn.silu(y_one_f).astype(jnp.bfloat16)
    patch_one = make_patches(act_one, 1)
    g_out = jnp.einsum("vtc,toc->vo", patch_one, weight_g, preferred_element_type=jnp.float32)
    x_two = (y_two.astype(jnp.float32) - g_out).astype(jnp.bfloat16)
    grad_g = jnp.einsum("vo,vti->oti", dy_two, patch_one, preferred_element_type=jnp.float32)
    back_two = make_patches(dy_two, -1)
    d_act_one = jnp.einsum("vto,toi->vi", back_two, weight_g, preferred_element_type=jnp.float32)
    dx_one = (dy_one.astype(jnp.float32) + d_act_one * silu_grad(y_one_f)).astype(jnp.bfloat16)
    return (x_two, dx_one, grad_g)


def half_f(inputs, x_two, dx_one, weight_f):
    y_one_f = inputs[0].astype(jnp.float32)
    dy_two = inputs[3]
    x_two_f = x_two.astype(jnp.float32)
    act_two = jax.nn.silu(x_two_f).astype(jnp.bfloat16)
    patch_two = make_patches(act_two, 1)
    f_out = jnp.einsum("vtc,toc->vo", patch_two, weight_f, preferred_element_type=jnp.float32)
    x_one = (y_one_f - f_out).astype(jnp.bfloat16)
    grad_f = jnp.einsum("vo,vti->oti", dx_one, patch_two, preferred_element_type=jnp.float32)
    back_one = make_patches(dx_one, -1)
    d_act_two = jnp.einsum("vto,toi->vi", back_one, weight_f, preferred_element_type=jnp.float32)
    dx_two = (dy_two.astype(jnp.float32) + d_act_two * silu_grad(x_two_f)).astype(jnp.bfloat16)
    return (x_one, dx_two, grad_f)


def body(incoming, feed, plan, weights, momentum):
    replicas = lax.axis_size("dp")
    is_last = lax.axis_index("section") == lax.axis_size("section") - 1
    weight = weights[0]
    current = incoming[0]
    results = []
    out_channels = weight.shape[2]
    in_channels = weight.shape[3]
    total_f = jnp.zeros((out_channels, 27, in_channels), jnp.float32)
    total_g = jnp.zeros((out_channels, 27, in_channels), jnp.float32)
    for tick in range(TICKS):
        x_two, dx_one, grad_g = half_g(current, weight[1])
        total_g = total_g + grad_g
        x_one, dx_two, grad_f = half_f(current, x_two, dx_one, weight[0])
        total_f = total_f + grad_f
        outs = jnp.stack([x_one, x_two, dx_one, dx_two])
        results.append(outs)
        if tick + 1 < TICKS:
            from_below = shifted(outs, "section", -1)
            chosen = lax.dynamic_index_in_dim(feed, plan[tick, 0], 0, keepdims=False)
            current = jnp.where(is_last, chosen, from_below)
    both = jnp.stack([total_f, total_g], axis=1).astype(jnp.bfloat16).astype(jnp.float32)
    shard_rows = lax.psum_scatter(
        both.astype(jnp.bfloat16), "dp", scatter_dimension=0, tiled=True
    ).astype(jnp.float32)
    shard_total = jnp.transpose(shard_rows, (1, 2, 0, 3))
    upstream = jnp.stack(results)[:, None]
    new_momentum = 0.9 * momentum[0] + shard_total / (replicas * TICKS)
    return (upstream, new_momentum[None])


def solution(mesh):
    in_specs = (
        P("section", None, "dp", None),
        P(None, None, "dp", None),
        P(None, "dp"),
        P("section", None, None, None, None),
        P("section", None, None, "dp", None),
    )
    out_specs = (P(None, "section", None, "dp", None), P("section", None, None, "dp", None))
    return jax.shard_map(body, mesh=mesh, in_specs=in_specs, out_specs=out_specs, check_vma=False)
```

profile of v0, /device:TPU:4, one launch (start us, length us, event | category | flops | bytes accessed | tf_op | source)
XLA Modules:
  0.0 186.6 jit_solution(5286013456155022090)
XLA Ops:
  7.2 0.9 slice_convert_fusion.1
  9.8 1.4 copy-done.4
  11.2 1.3 fusion.106
  15.1 1.3 fusion.99
  16.4 2.6 %collective-permute-start = (bf16[4,128,256]{2,1,0:T(8,128)(2,1)S(1)}, bf16[4,128,256]{2,1,0:T(8,128)(2,1)S(1)}, u32[]{:S(2)}, u32[]{:S(2)}) collective-permute-start(bf16[4,128,256]{2,1,0:T(8,128)(2,1)S(1)} %get-tuple-element.9), channel_id=1, source_target_pairs={{32,0},{64,32},{96,64},{128,96},{160,128},{192,160},{224,192},{33,... | collective-permute-start | bytes 786440 | tf_op jit(solution)/shard_map/ppermute | solution.py:15
  19.1 4.0 %fusion.146 = f32[256,27,256]{2,0,1:T(8,128)} fusion(bf16[128,27,256]{2,0,1:T(8,128)(2,1)S(1)} %constant_dynamic-update-slice_fusion.27, bf16[128,256]{1,0:T(8,128)(2,1)S(1)} %fusion.81), kind=kOutput, calls=%fused_computation.543 | convolution fusion | flops 452984832 | bytes 8912896 | tf_op jit(solution)/shard_map/vo,vti->oti/dot_general | solution.py:64
  23.7 1.1 fusion.143
  24.8 1.5 collective-permute-done
  26.4 1.0 bitcast_select_fusion
  28.4 0.8 slice-done.3
  29.2 1.3 fusion.112
  31.5 1.1 fusion.2
  33.1 1.2 copy-done
  34.3 1.0 slice-done.1
  35.2 2.8 %fusion.1 = bf16[256,1,27,256]{3,0,2,1:T(8,128)(2,1)} fusion(f32[256,27,256]{2,0,1:T(8,128)S(1)} %bitcast.524, bf16[128,27,256]{2,0,1:T(8,128)(2,1)S(1)} %constant_dynamic-update-slice_fusion.135, bf16[128,256]{1,0:T(8,128)(2,1)S(1)} %fusion.115), kind=kOutput, calls=%fused_computation.4 | convolution fusion | flops 456523776 | bytes 12451840 | tf_op jit(solution)/shard_map/vo,vti->oti/dot_general | solution.py:64
  38.1 2.6 %pad_maximum_fusion = bf16[256,2,27,256]{3,0,2,1:T(8,128)(2,1)S(1)} fusion(bf16[256,1,27,256]{3,0,2,1:T(8,128)(2,1)S(1)} %fusion.2, bf16[256,1,27,256]{3,0,2,1:T(8,128)(2,1)} %fusion.1), kind=kLoop, calls=%fused_computation | loop fusion | flops 3538944 | bytes 14155776 | tf_op jit(solution)/shard_map/stack | solution.py:92
  40.7 7.6 %copy.27 = bf16[256,2,27,256]{3,2,1,0:T(8,128)(2,1)} copy(bf16[256,2,27,256]{3,0,2,1:T(8,128)(2,1)S(1)} %pad_maximum_fusion) | data formatting | bytes 14155776
  48.3 11.3 %reshape.145 = bf16[256,13824]{1,0:T(8,128)(2,1)} reshape(bf16[256,2,27,256]{3,2,1,0:T(8,128)(2,1)} %copy.27) | data formatting | bytes 14155776
  60.2 1.1 copy-done.1
  61.2 3.3 %fusion.93 = bf16[1,128,256]{2,1,0:T(8,128)(2,1)S(1)} fusion(bf16[128,27,256]{2,0,1:T(8,128)(2,1)S(1)} %copy-done.1, bf16[1,2,27,256,256]{4,3,2,1,0:T(8,128)(2,1)} %param.8, bf16[4,128,256]{2,1,0:T(8,128)(2,1)S(1)} %bitcast_select_fusion), kind=kOutput, calls=%fused_computation.260 | convolution fusion | flops 453083136 | bytes 5439488 | tf_op jit(solution)/shard_map/vtc,toc->vo/dot_general | solution.py:62
  64.5 2.6 %fusion.139 = bf16[1,128,256]{2,1,0:T(8,128)(2,1)S(1)} fusion(bf16[128,256]{1,0:T(8,128)(2,1)S(1)} %get-tuple-element.7, bf16[128,27,256]{2,0,1:T(8,128)(2,1)S(1)} %constant_dynamic-update-slice_fusion.189, bf16[1,2,27,256,256]{4,3,2,1,0:T(8,128)(2,1)} %param.8, bf16[4,128,256]{2,1,0:T(8,128)(2,1)S(1)} %bitcast_select_fusion), kind=kOutput, calls=%fused_computation.536 | convolution fusion | flops 453378048 | bytes 5505024 | tf_op jit(solution)/shard_map/vto,toi->vi/dot_general | solution.py:66
  67.2 0.8 maximum_bitcast_fusion
  68.1 109.9 %reduce-scatter.4.cloned.1.call-done = bf16[8,13824]{1,0:T(8,128)(2,1)} async-done(((bf16[256,13824]{1,0:T(8,128)(2,1)}), bf16[8,13824]{1,0:T(8,128)(2,1)}) %reduce-scatter.4.cloned.1.call-update) | async-done | bytes 221200
  178.0 1.8 fusion.102
  (254 shorter events, 5.6 us)
Async XLA Ops:
  7.2 170.8 %reduce-scatter.4.cloned.1.call-start = ((), (), s32[]{:S(2)}) async-start(), calls=%async_computation.1 | async-start | bytes 7299072
  8.1 3.1 %copy-start.4 = (bf16[1,2,27,256,256]{4,3,2,1,0:T(8,128)(2,1)S(1)}, bf16[1,2,27,256,256]{4,3,2,1,0:T(8,128)(2,1)}, u32[]{:S(2)}) copy-start(bf16[1,2,27,256,256]{4,3,2,1,0:T(8,128)(2,1)} %param.8) | copy-start | bytes 21233668
  8.5 1.1 copy-start.3
  16.4 9.9 %collective-permute-start = (bf16[4,128,256]{2,1,0:T(8,128)(2,1)S(1)}, bf16[4,128,256]{2,1,0:T(8,128)(2,1)S(1)}, u32[]{:S(2)}, u32[]{:S(2)}) collective-permute-start(bf16[4,128,256]{2,1,0:T(8,128)(2,1)S(1)} %get-tuple-element.9), channel_id=1, source_target_pairs={{32,0},{64,32},{96,64},{128,96},{160,128},{192,160},{224,192},{33,... | collective-permute-start | bytes 786440 | tf_op jit(solution)/shard_map/ppermute | solution.py:15
  23.7 4.7 %slice-start.2 = ((s8[7077888]{0:T(1024)(128)(4,1)}), s8[4194304]{0:T(1024)(128)(4,1)S(1)}, s32[]{:S(2)}) async-start(s8[7077888]{0:T(1024)(128)(4,1)} %bitcast.752), calls=%async_computation.4 | async-start | bytes 8388608
  27.4 1.8 slice-start.3
  31.5 2.8 %slice-start = ((s8[7077888]{0:T(1024)(128)(4,1)}), s8[4194304]{0:T(1024)(128)(4,1)S(1)}, s32[]{:S(2)}) async-start(s8[7077888]{0:T(1024)(128)(4,1)} %bitcast.523), calls=%async_computation.2 | async-start | bytes 8388608
  31.5 3.7 %slice-start.1 = ((s8[7077888]{0:T(1024)(128)(4,1)}), s8[2883584]{0:T(1024)(128)(4,1)S(1)}, s32[]{:S(2)}) async-start(s8[7077888]{0:T(1024)(128)(4,1)} %bitcast.523), calls=%async_computation.3 | async-start | bytes 5767168
  33.1 1.2 copy-start
  59.8 1.5 copy-start.1
  67.2 110.8 %copy-start.2 = (f32[1,2,27,8,256]{4,3,2,1,0:T(8,128)S(1)}, f32[1,2,27,8,256]{4,3,2,1,0:T(8,128)}, u32[]{:S(2)}) copy-start(f32[1,2,27,8,256]{4,3,2,1,0:T(8,128)} %param.9) | copy-start | bytes 1327108
Sparse Core Ops, SparseCore 0:
  59.7 118.2 reduce-scatter.3
where the time goes:
time: 187 us
  waiting for transfers between devices  111 us (59%)
  local copies, waits for them, and re-layouts  27.5 us (15%)
  matrix products  20.8 us (11%)
  between operations  16.7 us (9%)
  other arithmetic  7.5 us (4%)
  starting transfers between devices  2.66 us (1%)
    unnamed x2, waiting for transfers between devices  110 us
    unnamed x221, local copies, waits for them, and re-layouts  26.4 us
    dot_general x2, matrix products, half_f(): jnp.einsum('vo,vti->oti', dx_one, patch_two, preferred_element_type=jnp.f...  6.82 us
    dot_general x2, matrix products, half_f(): jnp.einsum('vtc,toc->vo', patch_two, weight_f, preferred_element_type=jnp...  4.55 us
  transfers between devices with their start and end apart: 2, of which 2 were waited for; matrix products, arithmetic and copies ran while one was open for 7% of the time, Pallas kernels for 0%

commit v1 on v0

v1 whole, which is shorter than its diff:
```python
import functools

import jax
import jax.numpy as jnp
from jax import lax
from jax.experimental import pallas as pl
from jax.experimental.pallas import tpu as pltpu
from jax.sharding import PartitionSpec as P

TD, TH, TW = 2, 8, 8
VOX = TD * TH * TW
CH = 256
HALF = 128
LINE = TD * TW
TICKS = 2
NZ, NY, NC = 4, 4, 2
QUARTER = 64
F32, BF16 = jnp.float32, jnp.bfloat16
F, G = 0, 1
FIRST = {F: 1, G: 3}
SECOND = {F: 3, G: 1}
KEEP = {b: (0, SECOND[b]) for b in (F, G)}
SEND = {b: (FIRST[b], FIRST[b] ^ SECOND[b]) for b in (F, G)}
VMEM = pl.BlockSpec(memory_space=pltpu.VMEM)


def rank_of(z, y, c):
    return ((z % NZ) * NY + y % NY) * NC + c % NC


def dp_permute(array, move):
    pairs = []
    for z in range(NZ):
        for y in range(NY):
            for c in range(NC):
                pairs.append((rank_of(z, y, c), rank_of(*move(z, y, c))))
    return lax.ppermute(array, "dp", pairs)


def from_next_section(array):
    size = lax.axis_size("section")
    return lax.ppermute(array, "section", [(i, i - 1) for i in range(1, size)])


def to_hdw(x):
    return jnp.concatenate([x[64 * d + 8 * h : 64 * d + 8 * h + 8] for h in range(TH) for d in range(TD)], axis=0)


def to_dhw(x):
    return jnp.concatenate([x[16 * h + 8 * d : 16 * h + 8 * d + 8] for d in range(TD) for h in range(TH)], axis=0)


def silu_pair(u):
    sig = jax.nn.sigmoid(u)
    return u * sig, sig * (1.0 + u * (1.0 - sig))


def moved(x, dd, dw):
    row = lax.broadcasted_iota(jnp.int32, x.shape, 0)
    ok = None
    if dw:
        x = pltpu.roll(x, (-dw) % VOX, 0)
        w = row % TW + dw
        ok = (w >= 0) & (w < TW)
    if dd:
        pieces = [x[LINE * h + 8 * (1 - d) : LINE * h + 8 * (1 - d) + 8] for h in range(TH) for d in range(TD)]
        x = jnp.concatenate(pieces, axis=0)
        d = (row // TW) % TD + dd
        inside = (d >= 0) & (d < TD)
        ok = inside if ok is None else ok & inside
    if ok is not None:
        x = jnp.where(ok, x, 0.0)
    return x.astype(BF16)


def fill(buf, x, dd, sign):
    zero = jnp.zeros((LINE, CH), BF16)
    for dw in (-1, 0, 1):
        m = moved(x, sign * dd, sign * dw)
        for dh in (-1, 0, 1):
            k = 3 * (dh + 1) + dw + 1
            cols = slice(CH * k, CH * k + CH)
            if sign * dh == 0:
                buf[:, cols] = m
            elif sign * dh == 1:
                buf[: VOX - LINE, cols] = m[LINE:]
                buf[VOX - LINE :, cols] = zero
            else:
                buf[LINE:, cols] = m[: VOX - LINE]
                buf[:LINE, cols] = zero


def convolve(step, act, err, w_ref, buf_a, buf_e, acc_a, acc_e):
    for i, dd in enumerate((-1, 0, 1)):

        @pl.when(step == i)
        def _():
            fill(buf_a, act, dd, 1)
            fill(buf_e, err, dd, -1)

    ahead = None
    for k in range(9):
        term = lax.dot_general(
            buf_a[:, CH * k : CH * k + CH], w_ref[k], (((1,), (1,)), ((), ())), preferred_element_type=F32
        )
        ahead = term if ahead is None else ahead + term
    back = jnp.dot(buf_e[...], w_ref[...].reshape(9 * CH, CH), preferred_element_type=F32)

    @pl.when(step == 0)
    def _():
        acc_a[...] = ahead
        acc_e[...] = back

    @pl.when(step > 0)
    def _():
        acc_a[...] += ahead
        acc_e[...] += back


def pick(place, below, chosen):
    return jnp.where(place[3] == 1, chosen, below)


def half_g_kernel(place, *refs, picks):
    if picks:
        late, early, chosen, w_ref, out, give, mine, *scratch = refs
        y_one, dy_two, y_two, dy_one = (
            pick(place, late[0].astype(F32), chosen[0, 0].astype(F32)),
            pick(place, late[1].astype(F32), chosen[0, 3].astype(F32)),
            pick(place, early[0].astype(F32), chosen[0, 1].astype(F32)),
            pick(place, early[1].astype(F32), chosen[0, 2].astype(F32)),
        )
    else:
        incoming, w_ref, out, give, mine, *scratch = refs
        y_one, y_two, dy_one, dy_two = [incoming[i].astype(F32) for i in range(4)]
    step = pl.program_id(0)
    u = to_hdw(y_one)
    act, slope = silu_pair(u)
    act = act.astype(BF16).astype(F32)
    err = to_hdw(dy_two)
    convolve(step, act, err, w_ref, *scratch)
    acc_a, acc_e = scratch[2:]

    @pl.when(step == 2)
    def _():
        x_two = (to_hdw(y_two) - acc_a[...]).astype(BF16).astype(F32)
        dx_one = (to_hdw(dy_one) + acc_e[...] * slope).astype(BF16).astype(F32)
        out[0] = to_dhw(x_two).astype(BF16)
        out[1] = to_dhw(dx_one).astype(BF16)
        act_two = silu_pair(x_two)[0]
        core, y, z = place[0], place[1], place[2]
        for b, a, e in ((F, act_two, dx_one), (G, act, err)):
            low, high = a[:, :HALF], a[:, HALF:]
            mine[b] = jnp.where(core == 0, low, high).astype(BF16)
            give[b, :VOX] = jnp.where(core == 0, high, low).astype(BF16)
            flipped = e.T.astype(BF16)
            for zz in range(NZ):
                for yy in range(NY):
                    row = VOX + QUARTER * ((yy - y) & 3) + 16 * (zz ^ z)
                    start = QUARTER * zz + 16 * yy
                    give[b, pl.ds(pl.multiple_of(row, 16), 16)] = flipped[start : start + 16]


def half_f_kernel(place, *refs, picks):
    if picks:
        late, early, mid, chosen, first_early, first_late, w_ref, out, *scratch = refs
        y_one = pick(place, late[0].astype(F32), chosen[0, 0].astype(F32))
        dy_two = pick(place, late[1].astype(F32), chosen[0, 3].astype(F32))
    else:
        incoming, mid, w_ref, out, *scratch = refs
        y_one, dy_two = incoming[0].astype(F32), incoming[3].astype(F32)
    step = pl.program_id(0)
    x_two, dx_one = mid[0].astype(F32), mid[1].astype(F32)
    act, slope = silu_pair(to_hdw(x_two))
    act = act.astype(BF16).astype(F32)
    convolve(step, act, to_hdw(dx_one), w_ref, *scratch)
    acc_a, acc_e = scratch[2:]

    @pl.when(step == 2)
    def _():
        x_one = (y_one - to_dhw(acc_a[...])).astype(BF16)
        dx_two = (dy_two + to_dhw(acc_e[...] * slope)).astype(BF16)
        if picks:
            out[0, 0] = first_late[0]
            out[0, 1] = first_early[0]
            out[0, 2] = first_early[1]
            out[0, 3] = first_late[1]
            out[1, 0] = x_one
            out[1, 1] = mid[0]
            out[1, 2] = mid[1]
            out[1, 3] = dx_two
        else:
            out[0] = x_one
            out[1] = dx_two


def whole(shape):
    return pl.BlockSpec(shape, lambda i, place: (0,) * len(shape))


def call_half(kernel, place, args, weights, branch, out_shapes, picks, name):
    specs = []
    for a in args:
        if a.ndim == 4:
            specs.append(pl.BlockSpec((1,) + a.shape[1:], lambda i, place: (place[4], 0, 0, 0)))
        else:
            specs.append(whole(a.shape))
    specs.append(pl.BlockSpec((None, 9, CH, CH), lambda i, place: (branch, i, 0, 0)))
    single = len(out_shapes) == 1
    shapes = [jax.ShapeDtypeStruct(s, BF16) for s in out_shapes]
    result = pl.pallas_call(
        functools.partial(kernel, picks=picks),
        grid_spec=pltpu.PrefetchScalarGridSpec(
            num_scalar_prefetch=1,
            grid=(3,),
            in_specs=specs,
            out_specs=[whole(s) for s in out_shapes],
            scratch_shapes=[pltpu.VMEM((VOX, 9 * CH), BF16)] * 2 + [pltpu.VMEM((VOX, CH), F32)] * 2,
        ),
        out_shape=shapes,
        compiler_params=pltpu.CompilerParams(vmem_limit_bytes=20 << 20),
        cost_estimate=pl.CostEstimate(flops=4 * 27 * VOX * CH * CH, bytes_accessed=27 * CH * CH * 2, transcendentals=0),
        name=name,
    )(place, *args, weights)
    return result[0] if single else result


def pack_kernel(mine, give, got, *outs):
    for by, out in zip((1, 2, 3), outs):
        rows = slice(VOX + QUARTER * by, VOX + QUARTER * by + QUARTER)
        out[:, 0, :VOX] = mine[...]
        out[:, 0, VOX:] = give[:, rows]
        out[:, 1, :VOX] = got[:, :VOX]
        out[:, 1, VOX:] = got[:, rows]


def gather_factors(give, mine):
    got = dp_permute(give, lambda z, y, c: (z, y, c + 1))
    shape = jax.ShapeDtypeStruct((2, 2, VOX + QUARTER, HALF), BF16)
    packed = pl.pallas_call(
        pack_kernel,
        out_shape=[shape] * 3,
        in_specs=[VMEM] * 3,
        out_specs=[VMEM] * 3,
        compiler_params=pltpu.CompilerParams(vmem_limit_bytes=8 << 20),
        cost_estimate=pl.CostEstimate(flops=0, bytes_accessed=1 << 20, transcendentals=0),
        name="pack",
    )(mine, give, got)
    parts = [dp_permute(p, lambda z, y, c, by=by: (z, y + by, c)) for by, p in zip((1, 2, 3), packed)]
    return (mine, give, got, *parts)


def products(refs, branch, lhs, rhs):
    mine, give, got, *parts = refs
    tiles = [(mine[branch], give[branch, VOX : VOX + QUARTER]), (got[branch, :VOX], got[branch, VOX : VOX + QUARTER])]
    for p in parts:
        for tile in range(2):
            tiles.append((p[branch, tile, :VOX], p[branch, tile, VOX:]))
    lane = lax.broadcasted_iota(jnp.int32, (QUARTER, VOX), 1)
    depth, width = (lane // TW) % TD, lane % TW
    zero = jnp.zeros((LINE, HALF), BF16)
    for index, (act, err) in enumerate(tiles):
        at = VOX * index
        rhs[0, at : at + LINE] = zero
        rhs[0, at + LINE : at + VOX] = act[: VOX - LINE]
        rhs[1, at : at + VOX] = act
        rhs[2, at : at + VOX - LINE] = act[LINE:]
        rhs[2, at + VOX - LINE : at + VOX] = zero
        err = err.astype(F32)
        for dd in (-1, 0, 1):
            for dw in (-1, 0, 1):
                x = err
                if dd or dw:
                    x = pltpu.roll(err, (TW * dd + dw) % VOX, 1)
                    ok = (depth - dd >= 0) & (depth - dd < TD) & (width - dw >= 0) & (width - dw < TW)
                    x = jnp.where(ok, x, 0.0)
                v = 3 * (dd + 1) + dw + 1
                lhs[QUARTER * v : QUARTER * v + QUARTER, at : at + VOX] = x.astype(BF16)
    return [jnp.dot(lhs[...], rhs[dh], preferred_element_type=F32) for dh in range(3)]


def first_grads_kernel(*refs):
    *ins, out, lhs, rhs = refs
    for branch in (F, G):
        for dh, value in enumerate(products(ins, branch, lhs, rhs)):
            out[branch, dh] = value


def last_grads_kernel(*refs, branch):
    *ins, before, keep, send, lhs, rhs = refs
    for dh, value in enumerate(products(ins, branch, lhs, rhs)):
        value = (value + before[branch, dh]).astype(BF16)
        for dd in range(3):
            for dw in range(3):
                for slots, out in ((KEEP[branch], keep), (SEND[branch], send)):
                    for i, slot in enumerate(slots):
                        row = QUARTER * (3 * dd + dw) + 16 * slot
                        out[i, 9 * dd + 3 * dh + dw] = value[row : row + 16]


def grad_call(kernel, ins, out_shape, flops, name):
    return pl.pallas_call(
        kernel,
        out_shape=out_shape,
        in_specs=[VMEM] * len(ins),
        out_specs=jax.tree.map(lambda s: VMEM, out_shape),
        scratch_shapes=[pltpu.VMEM((9 * QUARTER, 8 * VOX), BF16), pltpu.VMEM((3, 8 * VOX, HALF), BF16)],
        compiler_params=pltpu.CompilerParams(vmem_limit_bytes=24 << 20),
        cost_estimate=pl.CostEstimate(flops=flops, bytes_accessed=4 << 20, transcendentals=0),
        name=name,
    )(*ins)


def middle_kernel(place, keep, got, mine, cross, same, chip):
    core = place[0]
    own = keep[0].astype(F32) + got[0].astype(F32)
    other = keep[1].astype(F32) + got[1].astype(F32)
    low, high = own[:, :8], own[:, 8:]
    mine[...] = jnp.where(core == 0, low, high)
    chip[...] = jnp.where(core == 0, high, low).astype(BF16)
    low, high = other[:, :8], other[:, 8:]
    same[...] = jnp.where(core == 0, low, high).astype(BF16)
    cross[...] = jnp.where(core == 0, high, low).astype(BF16)


def reduce_z(place, keep, send, branch):
    got = dp_permute(send, lambda z, y, c: (z ^ FIRST[branch], y, c))
    piece = (27, 8, HALF)
    mine, cross, same, chip = pl.pallas_call(
        middle_kernel,
        out_shape=[jax.ShapeDtypeStruct(piece, F32)] + [jax.ShapeDtypeStruct(piece, BF16)] * 3,
        in_specs=[pl.BlockSpec(memory_space=pltpu.SMEM), VMEM, VMEM],
        out_specs=[VMEM] * 4,
        compiler_params=pltpu.CompilerParams(vmem_limit_bytes=8 << 20),
        cost_estimate=pl.CostEstimate(flops=0, bytes_accessed=1 << 20, transcendentals=0),
        name=f"middle_{branch}",
    )(place, keep, got)
    same = dp_permute(same, lambda z, y, c: (z ^ SECOND[branch], y, c))
    cross = dp_permute(cross, lambda z, y, c: (z ^ SECOND[branch], y, c + 1))
    chip = dp_permute(chip, lambda z, y, c: (z, y, c + 1))
    return mine, same, cross, chip


def update_kernel(place, *refs, scale):
    *terms, momentum, out = refs
    core = place[0]
    for branch in (F, G):
        mine, same, cross, chip = terms[4 * branch : 4 * branch + 4]
        own = mine[...] + same[...].astype(F32)
        other = cross[...].astype(F32) + chip[...].astype(F32)
        low = jnp.where(core == 0, own, other)
        high = jnp.where(core == 0, other, own)
        out[branch, :, :, :HALF] = 0.9 * momentum[branch, :, :, :HALF] + low * scale
        out[branch, :, :, HALF:] = 0.9 * momentum[branch, :, :, HALF:] + high * scale


def body(incoming, feed, plan, weights, momentum):
    replicas = lax.axis_size("dp")
    rank = lax.axis_index("dp")
    z, y, c = rank // (NY * NC), (rank // NC) % NY, rank % NC
    is_last = (lax.axis_index("section") == lax.axis_size("section") - 1).astype(jnp.int32)
    slot = jnp.arange(8, dtype=jnp.int32)
    place = jnp.zeros((8,), jnp.int32)
    for i, value in enumerate((c, y, z, is_last, plan[0, 0])):
        place = jnp.where(slot == i, value, place)
    weights = weights[0]
    incoming = incoming[0]
    pair = (2, VOX, CH)
    mid_shapes = [pair, (2, VOX + CH, HALF), (2, VOX, HALF)]
    early, give, mine = call_half(half_g_kernel, place, [incoming], weights, G, mid_shapes, False, "half_g0")
    factors0 = gather_factors(give, mine)
    late = call_half(half_f_kernel, place, [incoming, early], weights, F, [pair], False, "half_f0")
    y_early, y_late = from_next_section(early), from_next_section(late)
    flops = 4 * 27 * QUARTER * HALF * 8 * VOX
    before = grad_call(
        first_grads_kernel, factors0, jax.ShapeDtypeStruct((2, 3, 9 * QUARTER, HALF), F32), flops, "grads0"
    )
    mid, give, mine = call_half(
        half_g_kernel, place, [y_late, y_early, feed], weights, G, mid_shapes, True, "half_g1"
    )
    factors1 = gather_factors(give, mine)
    upstream = call_half(
        half_f_kernel,
        place,
        [y_late, y_early, mid, feed, early, late],
        weights,
        F,
        [(2, 4, VOX, CH)],
        True,
        "half_f1",
    )
    terms = {}
    block = jax.ShapeDtypeStruct((2, 27, 16, HALF), BF16)
    for branch in (G, F):
        keep, send = grad_call(
            functools.partial(last_grads_kernel, branch=branch),
            (*factors1, before),
            [block, block],
            flops // 2,
            f"grads1_{branch}",
        )
        terms[branch] = reduce_z(place, keep, send, branch)
    new = pl.pallas_call(
        functools.partial(update_kernel, scale=1.0 / (replicas * TICKS)),
        out_shape=jax.ShapeDtypeStruct(momentum.shape[1:], F32),
        in_specs=[pl.BlockSpec(memory_space=pltpu.SMEM)] + [VMEM] * 9,
        out_specs=VMEM,
        compiler_params=pltpu.CompilerParams(vmem_limit_bytes=8 << 20),
        name="update",
    )(place, *terms[F], *terms[G], momentum[0])
    return (upstream[:, None], new[None])


def solution(mesh):
    in_specs = (
        P("section", None, "dp", None),
        P(None, None, "dp", None),
        P(None, "dp"),
        P("section", None, None, None, None),
        P("section", None, None, "dp", None),
    )
    out_specs = (P(None, "section", None, "dp", None), P("section", None, None, "dp", None))
    return jax.shard_map(body, mesh=mesh, in_specs=in_specs, out_specs=out_specs, check_vma=False)
```

time: 187 us -> 83 us (0.44)
  waiting for transfers between devices: 111 us -> 22.6 us
  starting transfers between devices: 2.66 us -> 32 us
  local copies, waits for them, and re-layouts: 27.5 us -> 3.97 us
  Pallas kernels: 0 us -> 21.9 us
  matrix products: 20.8 us -> 0 us
  between operations: 16.7 us -> 1.49 us
  other arithmetic: 7.5 us -> 0.01 us
    unnamed x2 -> x0, waiting for transfers between devices: 110 us -> none
    ppermute x1 -> x18, starting transfers between devices: 2.63 us -> 32 us  [the longest x16 25.4 us: dp_permute(): return lax.ppermute(array, 'dp', pairs)]
    unnamed x221 -> x12, local copies, waits for them, and re-layouts: 26.4 us -> 3.97 us
    pallas_call x0 -> x12, Pallas kernels: none -> 21.9 us  [the longest x4 14.5 us: call_half(): pl.pallas_call(functools.partial(kernel, picks=picks), grid_spec=pltpu.Pr...]
    ppermute x1 -> x18, waiting for transfers between devices: 1.53 us -> 22.6 us  [the longest x16 19.4 us: dp_permute(): return lax.ppermute(array, 'dp', pairs)]
    dot_general x12 -> x0, matrix products: 20.8 us -> none  [the longest x2 6.82 us: half_f(): jnp.einsum('vo,vti->oti', dx_one, patch_two, preferred_element_type=jnp.f...]
    another operation x3 -> x0, other arithmetic: 2.73 us -> none  [the longest x1 2.65 us: body(): jnp.stack([total_f, total_g], axis=1).astype(jnp.bfloat16)]
  transfers between devices with their start and end apart: 2 -> 18, of which waited for: 2 -> 9; matrix products, arithmetic and copies ran while one was open for 7% -> 0% of each run, Pallas kernels for 0% -> 15%
where the time goes in v1:
time: 83 us; the launch traced here: 81.9 us
  starting transfers between devices  32 us (39%)
  waiting for transfers between devices  22.6 us (27%)
  Pallas kernels  21.9 us (26%)
  local copies, waits for them, and re-layouts  3.97 us (5%)
  between operations  1.49 us (2%)
    ppermute x16, starting transfers between devices, dp_permute(): return lax.ppermute(array, 'dp', pairs)  25.4 us
    ppermute x16, waiting for transfers between devices, dp_permute(): return lax.ppermute(array, 'dp', pairs)  19.4 us
    pallas_call x4, Pallas kernels, call_half(): pl.pallas_call(functools.partial(kernel, picks=picks), grid_spec=pltpu.Pr...  14.5 us
    ppermute x2, starting transfers between devices, from_next_section(): return lax.ppermute(array, 'section', [(i, i - 1) for i in range(1, size)])  6.59 us
    pallas_call x3, Pallas kernels, grad_call(): pl.pallas_call(kernel, out_shape=out_shape, in_specs=[VMEM] * len(ins), o...  4.56 us
    unnamed x12, local copies, waits for them, and re-layouts  3.97 us
    ppermute x2, waiting for transfers between devices, from_next_section(): return lax.ppermute(array, 'section', [(i, i - 1) for i in range(1, size)])  3.23 us
  transfers between devices with their start and end apart: 18, of which 9 were waited for; matrix products, arithmetic and copies ran while one was open for 0% of the time, Pallas kernels for 15%

profile of v1, /device:TPU:4, one launch (start us, length us, event | category | flops | bytes accessed | tf_op | source)
XLA Modules:
  0.0 81.9 jit_solution(7341977374928565967)
XLA Ops:
  1.3 3.0 %copy-done = bf16[1,2,27,256,256]{4,3,2,1,0:T(8,128)(2,1)S(1)} copy-done((bf16[1,2,27,256,256]{4,3,2,1,0:T(8,128)(2,1)S(1)}, bf16[1,2,27,256,256]{4,3,2,1,0:T(8,128)(2,1)}, u32[]{:S(2)}) %copy-start) | copy-done | bytes 7077912
  5.3 3.4 %half_g0.1 = (bf16[2,128,256]{2,1,0:T(8,128)(2,1)S(1)}, bf16[2,384,128]{2,1,0:T(8,128)(2,1)S(1)}, bf16[2,128,128]{2,1,0:T(8,128)(2,1)S(1)}) custom-call(s32[8]{0:T(128)S(1)} %compare_select_fusion.4.place, bf16[4,128,256]{2,1,0:T(8,128)(2,1)S(1)} %bitcast.15, bf16[2,27,256,256]{3,2,1,0:T(8,128)(2,1)S(1)} %bitcast.9), custom_call_target="tpu_custom_call" | custom-call | flops 905969664 | bytes 3538944 | tf_op jit(solution)/shard_map/half_g0/pallas_call | solution.py:211
  8.8 3.3 %half_f0.1.refs_5_ = bf16[2,128,256]{2,1,0:T(8,128)(2,1)S(1)} custom-call(s32[8]{0:T(128)S(1)} %compare_select_fusion.4.place, bf16[4,128,256]{2,1,0:T(8,128)(2,1)S(1)} %bitcast.16, bf16[2,128,256]{2,1,0:T(8,128)(2,1)S(1)} %get-tuple-element.26.refs_1_.refs_4_, bf16[2,27,256,256]{3,2,1,0:T(8,128)(2,1)S(1)} %bitcast.10), custom_call_target="tpu_custom_call" | custom-call | flops 905969664 | bytes 3538944 | tf_op jit(solution)/shard_map/half_f0/pallas_call | solution.py:211
  12.1 2.4 %collective-permute-start = (bf16[2,128,256]{2,1,0:T(8,128)(2,1)S(1)}, bf16[2,128,256]{2,1,0:T(8,128)(2,1)S(1)}, u32[]{:S(2)}, u32[]{:S(2)}) collective-permute-start(bf16[2,128,256]{2,1,0:T(8,128)(2,1)S(1)} %half_f0.1.refs_5_), channel_id=1, source_target_pairs={{32,0},{64,32},{96,64},{128,96},{160,128},{192,160},{224,192},{33,... | collective-permute-start | bytes 393224 | tf_op jit(solution)/shard_map/ppermute | solution.py:42
  14.5 4.1 %collective-permute-start.1 = (bf16[2,128,256]{2,1,0:T(8,128)(2,1)S(1)}, bf16[2,128,256]{2,1,0:T(8,128)(2,1)S(1)}, u32[]{:S(2)}, u32[]{:S(2)}) collective-permute-start(bf16[2,128,256]{2,1,0:T(8,128)(2,1)S(1)} %get-tuple-element.26.refs_1_.refs_4_), channel_id=1, source_target_pairs={{32,0},{64,32},{96,64},{128,96},{160,128},{192,160},{224,192},{33,... | collective-permute-start | bytes 393224 | tf_op jit(solution)/shard_map/ppermute | solution.py:42
  19.9 2.2 %collective-permute-done.1.refs_1_ = bf16[2,128,256]{2,1,0:T(8,128)(2,1)S(1)} collective-permute-done((bf16[2,128,256]{2,1,0:T(8,128)(2,1)S(1)}, bf16[2,128,256]{2,1,0:T(8,128)(2,1)S(1)}, u32[]{:S(2)}, u32[]{:S(2)}) %collective-permute-start.1) | collective-permute-done | bytes 131104 | tf_op jit(solution)/shard_map/ppermute | solution.py:42
  22.0 3.6 %half_g1.1 = (bf16[2,128,256]{2,1,0:T(8,128)(2,1)S(1)}, bf16[2,384,128]{2,1,0:T(8,128)(2,1)S(1)}, bf16[2,128,128]{2,1,0:T(8,128)(2,1)S(1)}) custom-call(s32[8]{0:T(128)S(1)} %compare_select_fusion.4.place, bf16[2,128,256]{2,1,0:T(8,128)(2,1)S(1)} %collective-permute-done.refs_0_, bf16[2,128,256]{2,1,0:T(8,128)(2,1)S(1)} %collective-permute-done.1.refs_1_, ...), custom_call_target="tpu_custom_call" | custom-call | flops 905969664 | bytes 3538944 | tf_op jit(solution)/shard_map/half_g1/pallas_call | solution.py:211
  25.8 1.6 %collective-permute-start.7 = (bf16[2,2,192,128]{3,2,1,0:T(8,128)(2,1)S(1)}, bf16[2,2,192,128]{3,2,1,0:T(8,128)(2,1)S(1)}, u32[]{:S(2)}, u32[]{:S(2)}) collective-permute-start(bf16[2,2,192,128]{3,2,1,0:T(8,128)(2,1)S(1)} %get-tuple-element.35), channel_id=1, source_target_pairs={{0,2},{1,3},{2,4},{3,5},{4,6},{5,7},{6,0},{7,1},{8,10},{9,11},{10,... | collective-permute-start | bytes 589832 | tf_op jit(solution)/shard_map/ppermute | solution.py:37
  27.4 2.9 %collective-permute-start.8 = (bf16[2,2,192,128]{3,2,1,0:T(8,128)(2,1)S(1)}, bf16[2,2,192,128]{3,2,1,0:T(8,128)(2,1)S(1)}, u32[]{:S(2)}, u32[]{:S(2)}) collective-permute-start(bf16[2,2,192,128]{3,2,1,0:T(8,128)(2,1)S(1)} %get-tuple-element.36), channel_id=1, source_target_pairs={{0,4},{1,5},{2,6},{3,7},{4,0},{5,1},{6,2},{7,3},{8,12},{9,13},{10,... | collective-permute-start | bytes 589832 | tf_op jit(solution)/shard_map/ppermute | solution.py:37
  30.4 1.3 %collective-permute-start.9 = (bf16[2,2,192,128]{3,2,1,0:T(8,128)(2,1)S(1)}, bf16[2,2,192,128]{3,2,1,0:T(8,128)(2,1)S(1)}, u32[]{:S(2)}, u32[]{:S(2)}) collective-permute-start(bf16[2,2,192,128]{3,2,1,0:T(8,128)(2,1)S(1)} %get-tuple-element.37), channel_id=1, source_target_pairs={{0,6},{1,7},{2,0},{3,1},{4,2},{5,3},{6,4},{7,5},{8,14},{9,15},{10,... | collective-permute-start | bytes 589832 | tf_op jit(solution)/shard_map/ppermute | solution.py:37
  34.4 2.2 %collective-permute-start.5 = (bf16[2,2,192,128]{3,2,1,0:T(8,128)(2,1)S(1)}, bf16[2,2,192,128]{3,2,1,0:T(8,128)(2,1)S(1)}, u32[]{:S(2)}, u32[]{:S(2)}) collective-permute-start(bf16[2,2,192,128]{3,2,1,0:T(8,128)(2,1)S(1)} %get-tuple-element.32), channel_id=1, source_target_pairs={{0,6},{1,7},{2,0},{3,1},{4,2},{5,3},{6,4},{7,5},{8,14},{9,15},{10,... | collective-permute-start | bytes 589832 | tf_op jit(solution)/shard_map/ppermute | solution.py:37
  36.7 3.7 %collective-permute-done.8.refs_4_ = bf16[2,2,192,128]{3,2,1,0:T(8,128)(2,1)S(1)} collective-permute-done((bf16[2,2,192,128]{3,2,1,0:T(8,128)(2,1)S(1)}, bf16[2,2,192,128]{3,2,1,0:T(8,128)(2,1)S(1)}, u32[]{:S(2)}, u32[]{:S(2)}) %collective-permute-start.8) | collective-permute-done | bytes 196640 | tf_op jit(solution)/shard_map/ppermute | solution.py:37
  40.4 2.2 %grads0.1.refs_6_ = f32[2,3,576,128]{3,2,1,0:T(8,128)S(1)} custom-call(bf16[2,128,128]{2,1,0:T(8,128)(2,1)S(1)} %get-tuple-element.33.mine.refs_0_, bf16[2,384,128]{2,1,0:T(8,128)(2,1)S(1)} %get-tuple-element.34.give.refs_1_, bf16[2,384,128]{2,1,0:T(8,128)(2,1)S(1)} %collective-permute-done.6.got.refs_2_, ...), custom_call_target="tpu_custom_call" | custom-call | flops 905969664 | bytes 4194304 | tf_op jit(solution)/shard_map/grads0/pallas_call | solution.py:302
  43.7 4.6 %collective-permute-done.4.refs_4_ = bf16[2,2,192,128]{3,2,1,0:T(8,128)(2,1)S(1)} collective-permute-done((bf16[2,2,192,128]{3,2,1,0:T(8,128)(2,1)S(1)}, bf16[2,2,192,128]{3,2,1,0:T(8,128)(2,1)S(1)}, u32[]{:S(2)}, u32[]{:S(2)}) %collective-permute-start.4) | collective-permute-done | bytes 196640 | tf_op jit(solution)/shard_map/ppermute | solution.py:37
  48.3 1.2 %grads1_1.1 = (bf16[2,27,16,128]{3,2,1,0:T(8,128)(2,1)S(1)}, bf16[2,27,16,128]{3,2,1,0:T(8,128)(2,1)S(1)}) custom-call(bf16[2,128,128]{2,1,0:T(8,128)(2,1)S(1)} %get-tuple-element.28.mine.refs_0_, bf16[2,384,128]{2,1,0:T(8,128)(2,1)S(1)} %get-tuple-element.29.give.refs_1_, bf16[2,384,128]{2,1,0:T(8,128)(2,1)S(1)} %collective-permute-done.2.got.refs_2_, ...), custom_call_target="tpu_custom_call" | custom-call | flops 452984832 | bytes 4194304 | tf_op jit(solution)/shard_map/grads1_1/pallas_call | solution.py:302
  49.5 6.6 %collective-permute-start.14 = (bf16[2,27,16,128]{3,2,1,0:T(8,128)(2,1)S(1)}, bf16[2,27,16,128]{3,2,1,0:T(8,128)(2,1)S(1)}, u32[]{:S(2)}, u32[]{:S(2)}) collective-permute-start(bf16[2,27,16,128]{3,2,1,0:T(8,128)(2,1)S(1)} %get-tuple-element.45), channel_id=1, source_target_pairs={{0,24},{1,25},{2,26},{3,27},{4,28},{5,29},{6,30},{7,31},{8,16},{9,... | collective-permute-start | bytes 663560 | tf_op jit(solution)/shard_map/ppermute | solution.py:37
  56.1 1.2 %grads1_0.1 = (bf16[2,27,16,128]{3,2,1,0:T(8,128)(2,1)S(1)}, bf16[2,27,16,128]{3,2,1,0:T(8,128)(2,1)S(1)}) custom-call(bf16[2,128,128]{2,1,0:T(8,128)(2,1)S(1)} %get-tuple-element.28.mine.refs_0_, bf16[2,384,128]{2,1,0:T(8,128)(2,1)S(1)} %get-tuple-element.29.give.refs_1_, bf16[2,384,128]{2,1,0:T(8,128)(2,1)S(1)} %collective-permute-done.2.got.refs_2_, ...), custom_call_target="tpu_custom_call" | custom-call | flops 452984832 | bytes 4194304 | tf_op jit(solution)/shard_map/grads1_0/pallas_call | solution.py:302
  57.3 1.5 %collective-permute-start.10 = (bf16[2,27,16,128]{3,2,1,0:T(8,128)(2,1)S(1)}, bf16[2,27,16,128]{3,2,1,0:T(8,128)(2,1)S(1)}, u32[]{:S(2)}, u32[]{:S(2)}) collective-permute-start(bf16[2,27,16,128]{3,2,1,0:T(8,128)(2,1)S(1)} %get-tuple-element.39), channel_id=1, source_target_pairs={{0,8},{1,9},{2,10},{3,11},{4,12},{5,13},{6,14},{7,15},{8,0},{9,1},... | collective-permute-start | bytes 663560 | tf_op jit(solution)/shard_map/ppermute | solution.py:37
  58.8 6.5 %collective-permute-done.14.got = bf16[2,27,16,128]{3,2,1,0:T(8,128)(2,1)S(1)} collective-permute-done((bf16[2,27,16,128]{3,2,1,0:T(8,128)(2,1)S(1)}, bf16[2,27,16,128]{3,2,1,0:T(8,128)(2,1)S(1)}, u32[]{:S(2)}, u32[]{:S(2)}) %collective-permute-start.14) | collective-permute-done | bytes 221216 | tf_op jit(solution)/shard_map/ppermute | solution.py:37
  65.9 2.4 %collective-permute-start.15 = (bf16[27,8,128]{2,1,0:T(8,128)(2,1)S(1)}, bf16[27,8,128]{2,1,0:T(8,128)(2,1)S(1)}, u32[]{:S(2)}, u32[]{:S(2)}) collective-permute-start(bf16[27,8,128]{2,1,0:T(8,128)(2,1)S(1)} %get-tuple-element.47), channel_id=1, source_target_pairs={{0,8},{1,9},{2,10},{3,11},{4,12},{5,13},{6,14},{7,15},{8,0},{9,1},... | collective-permute-start | bytes 165896 | tf_op jit(solution)/shard_map/ppermute | solution.py:37
  70.6 3.8 %collective-permute-start.11 = (bf16[27,8,128]{2,1,0:T(8,128)(2,1)S(1)}, bf16[27,8,128]{2,1,0:T(8,128)(2,1)S(1)}, u32[]{:S(2)}, u32[]{:S(2)}) collective-permute-start(bf16[27,8,128]{2,1,0:T(8,128)(2,1)S(1)} %get-tuple-element.41), channel_id=1, source_target_pairs={{0,24},{1,25},{2,26},{3,27},{4,28},{5,29},{6,30},{7,31},{8,16},{9,... | collective-permute-start | bytes 165896 | tf_op jit(solution)/shard_map/ppermute | solution.py:37
  74.9 4.2 %half_f1.1 = bf16[2,4,128,256]{3,2,1,0:T(8,128)(2,1)} custom-call(s32[8]{0:T(128)S(1)} %compare_select_fusion.4.place, bf16[2,128,256]{2,1,0:T(8,128)(2,1)S(1)} %collective-permute-done.refs_0_, bf16[2,128,256]{2,1,0:T(8,128)(2,1)S(1)} %collective-permute-done.1.refs_1_, bf16[2,128,256]{2,1,0:T(8,128)(2,1)S(1)} %get-tuple-element.27.refs_2_, ...), custom_call_target="tpu_custom_call" | custom-call | flops 905969664 | bytes 3538944 | tf_op jit(solution)/shard_map/half_f1/pallas_call | solution.py:211
  79.1 1.4 %collective-permute-done.12.refs_2_ = bf16[27,8,128]{2,1,0:T(8,128)(2,1)S(1)} collective-permute-done((bf16[27,8,128]{2,1,0:T(8,128)(2,1)S(1)}, bf16[27,8,128]{2,1,0:T(8,128)(2,1)S(1)}, u32[]{:S(2)}, u32[]{:S(2)}) %collective-permute-start.12) | collective-permute-done | bytes 55328 | tf_op jit(solution)/shard_map/ppermute | solution.py:37
  80.5 1.4 %update.1 = f32[2,27,8,256]{3,2,1,0:T(8,128)} custom-call(s32[8]{0:T(128)S(1)} %compare_select_fusion.4.place, f32[27,8,128]{2,1,0:T(8,128)S(1)} %get-tuple-element.40.refs_0_, bf16[27,8,128]{2,1,0:T(8,128)(2,1)S(1)} %collective-permute-done.11.refs_1_, bf16[27,8,128]{2,1,0:T(8,128)(2,1)S(1)} %collective-permute-done.12.refs_2_, ...), custom_call_target="tpu_custom_call" | custom-call | tf_op jit(solution)/shard_map/update/pallas_call | solution.py:403
  (38 shorter events, 9.6 us)
Async XLA Ops:
  1.3 3.0 %copy-start = (bf16[1,2,27,256,256]{4,3,2,1,0:T(8,128)(2,1)S(1)}, bf16[1,2,27,256,256]{4,3,2,1,0:T(8,128)(2,1)}, u32[]{:S(2)}) copy-start(bf16[1,2,27,256,256]{4,3,2,1,0:T(8,128)(2,1)} %param.8) | copy-start | bytes 21233668
  4.3 0.9 %copy-start.2 = (bf16[1,4,128,256]{3,2,1,0:T(8,128)(2,1)S(1)}, bf16[1,4,128,256]{3,2,1,0:T(8,128)(2,1)}, u32[]{:S(2)}) copy-start(bf16[1,4,128,256]{3,2,1,0:T(8,128)(2,1)} %param.5) | copy-start | bytes 786436
  5.3 16.7 %slice-start = ((s8[7077888]{0:T(1024)(128)(4,1)}), s8[4194304]{0:T(1024)(128)(4,1)S(1)}, s32[]{:S(2)}) async-start(s8[7077888]{0:T(1024)(128)(4,1)} %bitcast.11), calls=%async_computation | async-start | bytes 8388608
  5.3 16.7 %copy-start.1 = (bf16[4,4,128,256]{3,2,1,0:T(8,128)(2,1)S(1)}, bf16[4,4,128,256]{3,2,1,0:T(8,128)(2,1)}, u32[]{:S(2)}) copy-start(bf16[4,4,128,256]{3,2,1,0:T(8,128)(2,1)} %refs_3_.1) | copy-start | bytes 3145732
  8.7 13.3 %slice-start.1 = ((s8[7077888]{0:T(1024)(128)(4,1)}), s8[2883584]{0:T(1024)(128)(4,1)S(1)}, s32[]{:S(2)}) async-start(s8[7077888]{0:T(1024)(128)(4,1)} %bitcast.11), calls=%async_computation.1 | async-start | bytes 5767168
  12.1 7.8 %collective-permute-start = (bf16[2,128,256]{2,1,0:T(8,128)(2,1)S(1)}, bf16[2,128,256]{2,1,0:T(8,128)(2,1)S(1)}, u32[]{:S(2)}, u32[]{:S(2)}) collective-permute-start(bf16[2,128,256]{2,1,0:T(8,128)(2,1)S(1)} %half_f0.1.refs_5_), channel_id=1, source_target_pairs={{32,0},{64,32},{96,64},{128,96},{160,128},{192,160},{224,192},{33,... | collective-permute-start | bytes 393224 | tf_op jit(solution)/shard_map/ppermute | solution.py:42
  14.5 7.5 %collective-permute-start.1 = (bf16[2,128,256]{2,1,0:T(8,128)(2,1)S(1)}, bf16[2,128,256]{2,1,0:T(8,128)(2,1)S(1)}, u32[]{:S(2)}, u32[]{:S(2)}) collective-permute-start(bf16[2,128,256]{2,1,0:T(8,128)(2,1)S(1)} %get-tuple-element.26.refs_1_.refs_4_), channel_id=1, source_target_pairs={{32,0},{64,32},{96,64},{128,96},{160,128},{192,160},{224,192},{33,... | collective-permute-start | bytes 393224 | tf_op jit(solution)/shard_map/ppermute | solution.py:42
  18.7 7.0 %collective-permute-start.6 = (bf16[2,384,128]{2,1,0:T(8,128)(2,1)S(1)}, bf16[2,384,128]{2,1,0:T(8,128)(2,1)S(1)}, u32[]{:S(2)}, u32[]{:S(2)}) collective-permute-start(bf16[2,384,128]{2,1,0:T(8,128)(2,1)S(1)} %get-tuple-element.34.give.refs_1_), channel_id=1, source_target_pairs={{0,1},{1,0},{2,3},{3,2},{4,5},{5,4},{6,7},{7,6},{8,9},{9,8},{10,11... | collective-permute-start | bytes 589832 | tf_op jit(solution)/shard_map/ppermute | solution.py:37
  25.6 6.1 %collective-permute-start.2 = (bf16[2,384,128]{2,1,0:T(8,128)(2,1)S(1)}, bf16[2,384,128]{2,1,0:T(8,128)(2,1)S(1)}, u32[]{:S(2)}, u32[]{:S(2)}) collective-permute-start(bf16[2,384,128]{2,1,0:T(8,128)(2,1)S(1)} %get-tuple-element.29.give.refs_1_), channel_id=1, source_target_pairs={{0,1},{1,0},{2,3},{3,2},{4,5},{5,4},{6,7},{7,6},{8,9},{9,8},{10,11... | collective-permute-start | bytes 589832 | tf_op jit(solution)/shard_map/ppermute | solution.py:37
  25.8 8.6 %collective-permute-start.7 = (bf16[2,2,192,128]{3,2,1,0:T(8,128)(2,1)S(1)}, bf16[2,2,192,128]{3,2,1,0:T(8,128)(2,1)S(1)}, u32[]{:S(2)}, u32[]{:S(2)}) collective-permute-start(bf16[2,2,192,128]{3,2,1,0:T(8,128)(2,1)S(1)} %get-tuple-element.35), channel_id=1, source_target_pairs={{0,2},{1,3},{2,4},{3,5},{4,6},{5,7},{6,0},{7,1},{8,10},{9,11},{10,... | collective-permute-start | bytes 589832 | tf_op jit(solution)/shard_map/ppermute | solution.py:37
  27.4 12.9 %collective-permute-start.8 = (bf16[2,2,192,128]{3,2,1,0:T(8,128)(2,1)S(1)}, bf16[2,2,192,128]{3,2,1,0:T(8,128)(2,1)S(1)}, u32[]{:S(2)}, u32[]{:S(2)}) collective-permute-start(bf16[2,2,192,128]{3,2,1,0:T(8,128)(2,1)S(1)} %get-tuple-element.36), channel_id=1, source_target_pairs={{0,4},{1,5},{2,6},{3,7},{4,0},{5,1},{6,2},{7,3},{8,12},{9,13},{10,... | collective-permute-start | bytes 589832 | tf_op jit(solution)/shard_map/ppermute | solution.py:37
  30.4 10.0 %collective-permute-start.9 = (bf16[2,2,192,128]{3,2,1,0:T(8,128)(2,1)S(1)}, bf16[2,2,192,128]{3,2,1,0:T(8,128)(2,1)S(1)}, u32[]{:S(2)}, u32[]{:S(2)}) collective-permute-start(bf16[2,2,192,128]{3,2,1,0:T(8,128)(2,1)S(1)} %get-tuple-element.37), channel_id=1, source_target_pairs={{0,6},{1,7},{2,0},{3,1},{4,2},{5,3},{6,4},{7,5},{8,14},{9,15},{10,... | collective-permute-start | bytes 589832 | tf_op jit(solution)/shard_map/ppermute | solution.py:37
  31.8 11.9 %collective-permute-start.3 = (bf16[2,2,192,128]{3,2,1,0:T(8,128)(2,1)S(1)}, bf16[2,2,192,128]{3,2,1,0:T(8,128)(2,1)S(1)}, u32[]{:S(2)}, u32[]{:S(2)}) collective-permute-start(bf16[2,2,192,128]{3,2,1,0:T(8,128)(2,1)S(1)} %get-tuple-element.30), channel_id=1, source_target_pairs={{0,2},{1,3},{2,4},{3,5},{4,6},{5,7},{6,0},{7,1},{8,10},{9,11},{10,... | collective-permute-start | bytes 589832 | tf_op jit(solution)/shard_map/ppermute | solution.py:37
  32.5 15.8 %collective-permute-start.4 = (bf16[2,2,192,128]{3,2,1,0:T(8,128)(2,1)S(1)}, bf16[2,2,192,128]{3,2,1,0:T(8,128)(2,1)S(1)}, u32[]{:S(2)}, u32[]{:S(2)}) collective-permute-start(bf16[2,2,192,128]{3,2,1,0:T(8,128)(2,1)S(1)} %get-tuple-element.31), channel_id=1, source_target_pairs={{0,4},{1,5},{2,6},{3,7},{4,0},{5,1},{6,2},{7,3},{8,12},{9,13},{10,... | collective-permute-start | bytes 589832 | tf_op jit(solution)/shard_map/ppermute | solution.py:37
  34.4 13.9 %collective-permute-start.5 = (bf16[2,2,192,128]{3,2,1,0:T(8,128)(2,1)S(1)}, bf16[2,2,192,128]{3,2,1,0:T(8,128)(2,1)S(1)}, u32[]{:S(2)}, u32[]{:S(2)}) collective-permute-start(bf16[2,2,192,128]{3,2,1,0:T(8,128)(2,1)S(1)} %get-tuple-element.32), channel_id=1, source_target_pairs={{0,6},{1,7},{2,0},{3,1},{4,2},{5,3},{6,4},{7,5},{8,14},{9,15},{10,... | collective-permute-start | bytes 589832 | tf_op jit(solution)/shard_map/ppermute | solution.py:37
  49.5 31.0 %copy-start.3 = (f32[1,2,27,8,256]{4,3,2,1,0:T(8,128)S(1)}, f32[1,2,27,8,256]{4,3,2,1,0:T(8,128)}, u32[]{:S(2)}) copy-start(f32[1,2,27,8,256]{4,3,2,1,0:T(8,128)} %param.9) | copy-start | bytes 1327108
  49.5 15.8 %collective-permute-start.14 = (bf16[2,27,16,128]{3,2,1,0:T(8,128)(2,1)S(1)}, bf16[2,27,16,128]{3,2,1,0:T(8,128)(2,1)S(1)}, u32[]{:S(2)}, u32[]{:S(2)}) collective-permute-start(bf16[2,27,16,128]{3,2,1,0:T(8,128)(2,1)S(1)} %get-tuple-element.45), channel_id=1, source_target_pairs={{0,24},{1,25},{2,26},{3,27},{4,28},{5,29},{6,30},{7,31},{8,16},{9,... | collective-permute-start | bytes 663560 | tf_op jit(solution)/shard_map/ppermute | solution.py:37
  57.3 12.6 %collective-permute-start.10 = (bf16[2,27,16,128]{3,2,1,0:T(8,128)(2,1)S(1)}, bf16[2,27,16,128]{3,2,1,0:T(8,128)(2,1)S(1)}, u32[]{:S(2)}, u32[]{:S(2)}) collective-permute-start(bf16[2,27,16,128]{3,2,1,0:T(8,128)(2,1)S(1)} %get-tuple-element.39), channel_id=1, source_target_pairs={{0,8},{1,9},{2,10},{3,11},{4,12},{5,13},{6,14},{7,15},{8,0},{9,1},... | collective-permute-start | bytes 663560 | tf_op jit(solution)/shard_map/ppermute | solution.py:37
  65.9 8.4 %collective-permute-start.15 = (bf16[27,8,128]{2,1,0:T(8,128)(2,1)S(1)}, bf16[27,8,128]{2,1,0:T(8,128)(2,1)S(1)}, u32[]{:S(2)}, u32[]{:S(2)}) collective-permute-start(bf16[27,8,128]{2,1,0:T(8,128)(2,1)S(1)} %get-tuple-element.47), channel_id=1, source_target_pairs={{0,8},{1,9},{2,10},{3,11},{4,12},{5,13},{6,14},{7,15},{8,0},{9,1},... | collective-permute-start | bytes 165896 | tf_op jit(solution)/shard_map/ppermute | solution.py:37
  68.3 10.8 %collective-permute-start.16 = (bf16[27,8,128]{2,1,0:T(8,128)(2,1)S(1)}, bf16[27,8,128]{2,1,0:T(8,128)(2,1)S(1)}, u32[]{:S(2)}, u32[]{:S(2)}) collective-permute-start(bf16[27,8,128]{2,1,0:T(8,128)(2,1)S(1)} %get-tuple-element.48), channel_id=1, source_target_pairs={{0,9},{1,8},{2,11},{3,10},{4,13},{5,12},{6,15},{7,14},{8,1},{9,0},... | collective-permute-start | bytes 165896 | tf_op jit(solution)/shard_map/ppermute | solution.py:37
  68.3 10.8 %collective-permute-start.17 = (bf16[27,8,128]{2,1,0:T(8,128)(2,1)S(1)}, bf16[27,8,128]{2,1,0:T(8,128)(2,1)S(1)}, u32[]{:S(2)}, u32[]{:S(2)}) collective-permute-start(bf16[27,8,128]{2,1,0:T(8,128)(2,1)S(1)} %get-tuple-element.49), channel_id=1, source_target_pairs={{0,1},{1,0},{2,3},{3,2},{4,5},{5,4},{6,7},{7,6},{8,9},{9,8},{10,11... | collective-permute-start | bytes 165896 | tf_op jit(solution)/shard_map/ppermute | solution.py:37
  70.6 8.6 %collective-permute-start.11 = (bf16[27,8,128]{2,1,0:T(8,128)(2,1)S(1)}, bf16[27,8,128]{2,1,0:T(8,128)(2,1)S(1)}, u32[]{:S(2)}, u32[]{:S(2)}) collective-permute-start(bf16[27,8,128]{2,1,0:T(8,128)(2,1)S(1)} %get-tuple-element.41), channel_id=1, source_target_pairs={{0,24},{1,25},{2,26},{3,27},{4,28},{5,29},{6,30},{7,31},{8,16},{9,... | collective-permute-start | bytes 165896 | tf_op jit(solution)/shard_map/ppermute | solution.py:37
  74.3 6.2 %collective-permute-start.12 = (bf16[27,8,128]{2,1,0:T(8,128)(2,1)S(1)}, bf16[27,8,128]{2,1,0:T(8,128)(2,1)S(1)}, u32[]{:S(2)}, u32[]{:S(2)}) collective-permute-start(bf16[27,8,128]{2,1,0:T(8,128)(2,1)S(1)} %get-tuple-element.42), channel_id=1, source_target_pairs={{0,25},{1,24},{2,27},{3,26},{4,29},{5,28},{6,31},{7,30},{8,17},{9,... | collective-permute-start | bytes 165896 | tf_op jit(solution)/shard_map/ppermute | solution.py:37
  74.4 6.2 %collective-permute-start.13 = (bf16[27,8,128]{2,1,0:T(8,128)(2,1)S(1)}, bf16[27,8,128]{2,1,0:T(8,128)(2,1)S(1)}, u32[]{:S(2)}, u32[]{:S(2)}) collective-permute-start(bf16[27,8,128]{2,1,0:T(8,128)(2,1)S(1)} %get-tuple-element.43), channel_id=1, source_target_pairs={{0,1},{1,0},{2,3},{3,2},{4,5},{5,4},{6,7},{7,6},{8,9},{9,8},{10,11... | collective-permute-start | bytes 165896 | tf_op jit(solution)/shard_map/ppermute | solution.py:37

commit v2 on v1

v2 whole, which is shorter than its diff:
```python
import functools

import jax
import jax.numpy as jnp
from jax import lax
from jax.experimental import pallas as pl
from jax.experimental.pallas import tpu as pltpu
from jax.sharding import PartitionSpec as P


TD, TH, TW = 2, 8, 8
VOX = TD * TH * TW
CH = 256
HALF = 128
LINE = TD * TW
TICKS = 2
NZ, NY, NC = 4, 4, 2
QUARTER = 64
F32, BF16 = jnp.float32, jnp.bfloat16
F, G = 0, 1
FIRST = {F: 1, G: 3}
SECOND = {F: 3, G: 1}
KEEP = {b: (0, SECOND[b]) for b in (F, G)}
SEND = {b: (FIRST[b], FIRST[b] ^ SECOND[b]) for b in (F, G)}
CHUNKS = 3
VMEM = pl.BlockSpec(memory_space=pltpu.VMEM)
SMEM = pl.BlockSpec(memory_space=pltpu.SMEM)
HBM = pl.BlockSpec(memory_space=pltpu.HBM)


def rank_of(z, y, c):
    return ((z % NZ) * NY + y % NY) * NC + c % NC


def dp_permute(array, move):
    pairs = []
    for z in range(NZ):
        for y in range(NY):
            for c in range(NC):
                pairs.append((rank_of(z, y, c), rank_of(*move(z, y, c))))
    return lax.ppermute(array, "dp", pairs)


def from_next_section(array):
    size = lax.axis_size("section")
    return lax.ppermute(array, "section", [(i, i - 1) for i in range(1, size)])


def to_hdw(x):
    return jnp.concatenate([x[64 * d + 8 * h : 64 * d + 8 * h + 8] for h in range(TH) for d in range(TD)], axis=0)


def to_dhw(x):
    return jnp.concatenate([x[16 * h + 8 * d : 16 * h + 8 * d + 8] for d in range(TD) for h in range(TH)], axis=0)


def silu_pair(u):
    sig = jax.nn.sigmoid(u)
    return u * sig, sig * (1.0 + u * (1.0 - sig))


def moved(x, dd, dw):
    row = lax.broadcasted_iota(jnp.int32, x.shape, 0)
    ok = None
    if dw:
        x = pltpu.roll(x, (-dw) % VOX, 0)
        w = row % TW + dw
        ok = (w >= 0) & (w < TW)
    if dd:
        pieces = [x[LINE * h + 8 * (1 - d) : LINE * h + 8 * (1 - d) + 8] for h in range(TH) for d in range(TD)]
        x = jnp.concatenate(pieces, axis=0)
        d = (row // TW) % TD + dd
        inside = (d >= 0) & (d < TD)
        ok = inside if ok is None else ok & inside
    if ok is not None:
        x = jnp.where(ok, x, 0.0)
    return x.astype(BF16)


def fill(buf, x, sign):
    zero = jnp.zeros((LINE, CH), BF16)
    for dd in (-1, 0, 1):
        for dw in (-1, 0, 1):
            m = moved(x, sign * dd, sign * dw)
            for dh in (-1, 0, 1):
                t = 9 * (dd + 1) + 3 * (dh + 1) + dw + 1
                cols = slice(CH * t, CH * t + CH)
                if sign * dh == 0:
                    buf[:, cols] = m
                elif sign * dh == 1:
                    buf[: VOX - LINE, cols] = m[LINE:]
                    buf[VOX - LINE :, cols] = zero
                else:
                    buf[LINE:, cols] = m[: VOX - LINE]
                    buf[:LINE, cols] = zero


def convolve(act, err, wait, w_ref, buf_a, buf_e):
    fill(buf_a, act, 1)
    fill(buf_e, err, -1)
    wait()
    back = jnp.dot(buf_e[...], w_ref[...].reshape(27 * CH, CH), preferred_element_type=F32)
    ahead = None
    for t in range(27):
        term = lax.dot_general(
            buf_a[:, CH * t : CH * t + CH], w_ref[t], (((1,), (1,)), ((), ())), preferred_element_type=F32
        )
        ahead = term if ahead is None else ahead + term
    return ahead, back


def pick(place, below, chosen):
    return jnp.where(place[3] == 1, chosen, below)


def fetches(w_hbm, w_vmem, branch, sems):
    size = 27 // CHUNKS
    copies = []
    for k in range(CHUNKS):
        taps = pl.ds(size * k, size)
        copies.append(pltpu.make_async_copy(w_hbm.at[branch, taps], w_vmem.at[taps], sems.at[CHUNKS * branch + k]))
    return copies


def half_g_kernel(place, *refs, picks):
    if picks:
        late, early, feed, w_g, out, give, mine, *bufs = refs
        chosen = feed.at[place[4]]
        y_one, dy_two, y_two, dy_one = (
            pick(place, late[0].astype(F32), chosen[0].astype(F32)),
            pick(place, late[1].astype(F32), chosen[3].astype(F32)),
            pick(place, early[0].astype(F32), chosen[1].astype(F32)),
            pick(place, early[1].astype(F32), chosen[2].astype(F32)),
        )

        def wait():
            pass

    else:
        incoming, w_hbm, out, give, mine, held, w_g, w_f, *bufs, sems = refs
        first = pltpu.make_async_copy(incoming, held, sems.at[2 * CHUNKS])
        first.start()
        copies_g, copies_f = fetches(w_hbm, w_g, G, sems), fetches(w_hbm, w_f, F, sems)
        for copy in copies_g:
            copy.start()
        first.wait()
        y_one, y_two, dy_one, dy_two = [held[i].astype(F32) for i in range(4)]

        def wait():
            for copy in copies_g:
                copy.wait()
            for copy in copies_f:
                copy.start()

    u = to_hdw(y_one)
    act, slope = silu_pair(u)
    act = act.astype(BF16).astype(F32)
    err = to_hdw(dy_two)
    ahead, back = convolve(act, err, wait, w_g, *bufs)
    x_two = (to_hdw(y_two) - ahead).astype(BF16).astype(F32)
    dx_one = (to_hdw(dy_one) + back * slope).astype(BF16).astype(F32)
    out[0] = to_dhw(x_two).astype(BF16)
    out[1] = to_dhw(dx_one).astype(BF16)
    act_two = silu_pair(x_two)[0]
    core, y, z = place[0], place[1], place[2]
    for b, a, e in ((F, act_two, dx_one), (G, act, err)):
        low, high = a[:, :HALF], a[:, HALF:]
        mine[b] = jnp.where(core == 0, low, high).astype(BF16)
        give[b, :VOX] = jnp.where(core == 0, high, low).astype(BF16)
        flipped = e.T.astype(BF16)
        for zz in range(NZ):
            for yy in range(NY):
                row = VOX + QUARTER * ((yy - y) & 3) + 16 * (zz ^ z)
                start = QUARTER * zz + 16 * yy
                give[b, pl.ds(pl.multiple_of(row, 16), 16)] = flipped[start : start + 16]
    if not picks:
        for copy in copies_f:
            copy.wait()


def half_f_kernel(place, *refs, picks):
    if picks:
        late, early, mid, feed, first_early, first_late, w_f, out, *bufs = refs
        chosen = feed.at[place[4]]
        y_one = pick(place, late[0].astype(F32), chosen[0].astype(F32))
        dy_two = pick(place, late[1].astype(F32), chosen[3].astype(F32))
    else:
        held, mid, w_f, out, *bufs = refs
        y_one, dy_two = held[0].astype(F32), held[3].astype(F32)
    x_two, dx_one = mid[0].astype(F32), mid[1].astype(F32)
    act, slope = silu_pair(to_hdw(x_two))
    act = act.astype(BF16).astype(F32)
    ahead, back = convolve(act, to_hdw(dx_one), lambda: None, w_f, *bufs)
    x_one = (y_one - to_dhw(ahead)).astype(BF16)
    dx_two = (dy_two + to_dhw(back * slope)).astype(BF16)
    if picks:
        out[0, 0] = first_late[0]
        out[0, 1] = first_early[0]
        out[0, 2] = first_early[1]
        out[0, 3] = first_late[1]
        out[1, 0] = x_one
        out[1, 1] = mid[0]
        out[1, 2] = mid[1]
        out[1, 3] = dx_two
    else:
        out[0] = x_one
        out[1] = dx_two


def call_half(kernel, place, args, out_shapes, picks, in_hbm=False):
    scratch = [pltpu.VMEM((VOX, 27 * CH), BF16)] * 2
    return pl.pallas_call(
        functools.partial(kernel, picks=picks),
        in_specs=[SMEM] + [HBM if in_hbm else VMEM] * len(args),
        out_specs=[VMEM] * len(out_shapes),
        scratch_shapes=scratch + ([pltpu.SemaphoreType.DMA((2 * CHUNKS + 1,))] if in_hbm else []),
        out_shape=[jax.ShapeDtypeStruct(s, BF16) for s in out_shapes],
        compiler_params=pltpu.CompilerParams(vmem_limit_bytes=20 << 20),
        cost_estimate=pl.CostEstimate(flops=4 * 27 * VOX * CH * CH, bytes_accessed=27 * CH * CH * 2, transcendentals=0),
    )(place, *args)


def pack_kernel(mine, give, got, *outs, groups):
    at = 0
    for branches in groups:
        for by in (1, 2, 3):
            out = outs[at]
            at += 1
            rows = slice(VOX + QUARTER * by, VOX + QUARTER * by + QUARTER)
            for i, b in enumerate(branches):
                out[i, 0, :VOX] = mine[b]
                out[i, 0, VOX:] = give[b, rows]
                out[i, 1, :VOX] = got[b, :VOX]
                out[i, 1, VOX:] = got[b, rows]


def gather_factors(give, mine, groups):
    got = dp_permute(give, lambda z, y, c: (z, y, c + 1))
    shapes = [
        jax.ShapeDtypeStruct((len(branches), 2, VOX + QUARTER, HALF), BF16) for branches in groups for _ in range(3)
    ]
    packed = pl.pallas_call(
        functools.partial(pack_kernel, groups=groups),
        out_shape=shapes,
        in_specs=[VMEM] * 3,
        out_specs=[VMEM] * len(shapes),
        compiler_params=pltpu.CompilerParams(vmem_limit_bytes=8 << 20),
        cost_estimate=pl.CostEstimate(flops=0, bytes_accessed=1 << 20, transcendentals=0),
    )(mine, give, got)
    parts = []
    for n in range(len(groups)):
        for by in (1, 2, 3):
            message = packed[3 * n + by - 1]
            parts.append(dp_permute(message, lambda z, y, c, by=by: (z, y + by, c)))
    return [(mine, give, got, *parts[3 * n : 3 * n + 3]) for n in range(len(groups))]


def products(refs, branch, at_part, lhs, rhs):
    mine, give, got, *parts = refs
    tiles = [(mine[branch], give[branch, VOX : VOX + QUARTER]), (got[branch, :VOX], got[branch, VOX : VOX + QUARTER])]
    for p in parts:
        for tile in range(2):
            tiles.append((p[at_part, tile, :VOX], p[at_part, tile, VOX:]))
    lane = lax.broadcasted_iota(jnp.int32, (QUARTER, VOX), 1)
    depth, width = (lane // TW) % TD, lane % TW
    zero = jnp.zeros((LINE, HALF), BF16)
    for index, (act, err) in enumerate(tiles):
        at = VOX * index
        rhs[0, at : at + LINE] = zero
        rhs[0, at + LINE : at + VOX] = act[: VOX - LINE]
        rhs[1, at : at + VOX] = act
        rhs[2, at : at + VOX - LINE] = act[LINE:]
        rhs[2, at + VOX - LINE : at + VOX] = zero
        err = err.astype(F32)
        for dd in (-1, 0, 1):
            for dw in (-1, 0, 1):
                x = err
                if dd or dw:
                    x = pltpu.roll(err, (TW * dd + dw) % VOX, 1)
                    ok = (depth - dd >= 0) & (depth - dd < TD) & (width - dw >= 0) & (width - dw < TW)
                    x = jnp.where(ok, x, 0.0)
                v = 3 * (dd + 1) + dw + 1
                lhs[QUARTER * v : QUARTER * v + QUARTER, at : at + VOX] = x.astype(BF16)
    return [jnp.dot(lhs[...], rhs[dh], preferred_element_type=F32) for dh in range(3)]


def first_grads_kernel(*refs):
    *ins, out, lhs, rhs = refs
    for branch in (F, G):
        for dh, value in enumerate(products(ins, branch, branch, lhs, rhs)):
            out[branch, dh] = value


def last_grads_kernel(*refs, branch):
    *ins, before, keep, send, lhs, rhs = refs
    for dh, value in enumerate(products(ins, branch, branch, lhs, rhs)):
        value = (value + before[branch, dh]).astype(BF16)
        for dd in range(3):
            for dw in range(3):
                for slots, out in ((KEEP[branch], keep), (SEND[branch], send)):
                    for i, slot in enumerate(slots):
                        row = QUARTER * (3 * dd + dw) + 16 * slot
                        out[i, 9 * dd + 3 * dh + dw] = value[row : row + 16]


def grad_call(kernel, ins, out_shape, flops):
    return pl.pallas_call(
        kernel,
        out_shape=out_shape,
        in_specs=[VMEM] * len(ins),
        out_specs=jax.tree.map(lambda s: VMEM, out_shape),
        scratch_shapes=[pltpu.VMEM((9 * QUARTER, 8 * VOX), BF16), pltpu.VMEM((3, 8 * VOX, HALF), BF16)],
        compiler_params=pltpu.CompilerParams(vmem_limit_bytes=24 << 20),
        cost_estimate=pl.CostEstimate(flops=flops, bytes_accessed=4 << 20, transcendentals=0),
    )(*ins)


def small_call(kernel, ins, out_shape):
    return pl.pallas_call(
        kernel,
        out_shape=out_shape,
        in_specs=ins[0],
        out_specs=jax.tree.map(lambda s: VMEM, out_shape),
        compiler_params=pltpu.CompilerParams(vmem_limit_bytes=8 << 20),
        cost_estimate=pl.CostEstimate(flops=0, bytes_accessed=1 << 20, transcendentals=0),
    )(*ins[1])


def middle_kernel(keep, got, own, other):
    own[...] = keep[0].astype(F32) + got[0].astype(F32)
    other[...] = (keep[1].astype(F32) + got[1].astype(F32)).astype(BF16)


def reduce_z(keep, send, branch):
    got = dp_permute(send, lambda z, y, c: (z ^ FIRST[branch], y, c))
    piece = (27, 16, HALF)
    own, other = small_call(
        middle_kernel, ([VMEM] * 2, (keep, got)), [jax.ShapeDtypeStruct(piece, F32), jax.ShapeDtypeStruct(piece, BF16)]
    )
    return own, dp_permute(other, lambda z, y, c: (z ^ SECOND[branch], y, c))


def total_kernel(place, own_f, last_f, own_g, last_g, mine, give):
    first = place[0] == 0
    for branch, own, last in ((F, own_f, last_f), (G, own_g, last_g)):
        total = own[...] + last[...].astype(F32)
        low, high = total[:, :8], total[:, 8:]
        mine[branch] = jnp.where(first, low, high)
        give[branch] = jnp.where(first, high, low).astype(BF16)


def update_kernel(place, mine, got, momentum, out, *, scale):
    first = place[0] == 0
    for branch in (F, G):
        own, other = mine[branch], got[branch].astype(F32)
        low = jnp.where(first, own, other)
        high = jnp.where(first, other, own)
        out[branch, :, :, :HALF] = 0.9 * momentum[branch, :, :, :HALF] + low * scale
        out[branch, :, :, HALF:] = 0.9 * momentum[branch, :, :, HALF:] + high * scale


def steps(incoming, feed, plan, weights, momentum):
    replicas = lax.axis_size("dp")
    rank = lax.axis_index("dp")
    z, y, c = rank // (NY * NC), (rank // NC) % NY, rank % NC
    is_last = (lax.axis_index("section") == lax.axis_size("section") - 1).astype(jnp.int32)
    slot = jnp.arange(8, dtype=jnp.int32)
    place = jnp.zeros((8,), jnp.int32)
    for i, value in enumerate((c, y, z, is_last, plan[0, 0])):
        place = jnp.where(slot == i, value, place)
    weights = pltpu.with_memory_space_constraint(weights[0], pltpu.HBM)
    incoming = pltpu.with_memory_space_constraint(incoming[0], pltpu.HBM)
    pair = (2, VOX, CH)
    mid_shapes = [pair, (2, VOX + CH, HALF), (2, VOX, HALF)]
    early, give, mine, held, w_g, w_f = call_half(
        half_g_kernel,
        place,
        [incoming, weights],
        [*mid_shapes, (4, VOX, CH), (27, CH, CH), (27, CH, CH)],
        False,
        in_hbm=True,
    )
    (factors0,) = gather_factors(give, mine, ((F, G),))
    (late,) = call_half(half_f_kernel, place, [held, early, w_f], [pair], False)
    y_early, y_late = from_next_section(early), from_next_section(late)
    flops = 4 * 27 * QUARTER * HALF * 8 * VOX
    before = grad_call(first_grads_kernel, factors0, jax.ShapeDtypeStruct((2, 3, 9 * QUARTER, HALF), F32), flops)
    mid, give, mine = call_half(half_g_kernel, place, [y_late, y_early, feed, w_g], mid_shapes, True)
    (factors1,) = gather_factors(give, mine, ((F, G),))
    (upstream,) = call_half(
        half_f_kernel, place, [y_late, y_early, mid, feed, early, late, w_f], [(2, 4, VOX, CH)], True
    )
    terms = {}
    block = jax.ShapeDtypeStruct((2, 27, 16, HALF), BF16)
    for branch in (G, F):
        keep, send = grad_call(
            functools.partial(last_grads_kernel, branch=branch), (*factors1, before), [block, block], flops // 2
        )
        terms[branch] = reduce_z(keep, send, branch)
    piece = (2, 27, 8, HALF)
    mine, give = small_call(
        total_kernel,
        ([SMEM] + [VMEM] * 4, (place, *terms[F], *terms[G])),
        [jax.ShapeDtypeStruct(piece, F32), jax.ShapeDtypeStruct(piece, BF16)],
    )
    got = dp_permute(give, lambda z, y, c: (z, y, 1 - c))
    new = small_call(
        functools.partial(update_kernel, scale=1.0 / (replicas * TICKS)),
        ([SMEM] + [VMEM] * 3, (place, mine, got, momentum[0])),
        jax.ShapeDtypeStruct(momentum.shape[1:], F32),
    )
    return (upstream[:, None], new[None])


def solution(mesh):
    in_specs = (
        P("section", None, "dp", None),
        P(None, None, "dp", None),
        P(None, "dp"),
        P("section", None, None, None, None),
        P("section", None, None, "dp", None),
    )
    out_specs = (P(None, "section", None, "dp", None), P("section", None, None, "dp", None))
    return jax.shard_map(steps, mesh=mesh, in_specs=in_specs, out_specs=out_specs, check_vma=False)
```

time: 83 us -> 81.5 us (0.982)
  the two profiles are of different devices: /device:TPU:4 before, /device:TPU:1 now
where the time goes in v2:
time: 81.5 us; the launch traced here: 81.3 us
  waiting for transfers between devices  30.7 us (38%)
  starting transfers between devices  30.4 us (37%)
  Pallas kernels  18.7 us (23%)
  between operations  1.45 us (2%)
    ppermute x13, waiting for transfers between devices, dp_permute(): return lax.ppermute(array, 'dp', pairs)  27.9 us
    ppermute x13, starting transfers between devices, dp_permute(): return lax.ppermute(array, 'dp', pairs)  27.8 us
    pallas_call x4, Pallas kernels, call_half(): pl.pallas_call(functools.partial(kernel, picks=picks), in_specs=[SMEM] +...  11.9 us
    pallas_call x3, Pallas kernels, grad_call(): pl.pallas_call(kernel, out_shape=out_shape, in_specs=[VMEM] * len(ins), o...  4.55 us
    ppermute x2, waiting for transfers between devices, from_next_section(): return lax.ppermute(array, 'section', [(i, i - 1) for i in range(1, size)])  2.87 us
    ppermute x2, starting transfers between devices, from_next_section(): return lax.ppermute(array, 'section', [(i, i - 1) for i in range(1, size)])  2.58 us
    pallas_call x4, Pallas kernels, small_call(): pl.pallas_call(kernel, out_shape=out_shape, in_specs=ins[0], out_specs=ja...  2.08 us
  transfers between devices with their start and end apart: 15, of which 10 were waited for; matrix products, arithmetic and copies ran while one was open for 0% of the time, Pallas kernels for 11%

profile of v2, /device:TPU:1, one launch (start us, length us, event | category | flops | bytes accessed | tf_op | source)
XLA Modules:
  0.0 81.3 jit_solution(12242885676538077855)
XLA Ops:
  1.3 4.7 %shard_map.68 = (bf16[2,128,256]{2,1,0:T(8,128)(2,1)S(1)}, bf16[2,384,128]{2,1,0:T(8,128)(2,1)S(1)}, bf16[2,128,128]{2,1,0:T(8,128)(2,1)S(1)}, bf16[4,128,256]{2...) custom-call(s32[8]{0:T(128)S(1)} %compare_select_fusion.4.place, ...), custom_call_target="tpu_custom_call" | custom-call | flops 905969664 | bytes 3538944 | tf_op jit(solution)/shard_map/pallas_call | solution.py:212
  6.0 2.2 %shard_map.69.refs_5_ = bf16[2,128,256]{2,1,0:T(8,128)(2,1)S(1)} custom-call(s32[8]{0:T(128)S(1)} %compare_select_fusion.4.place, bf16[4,128,256]{2,1,0:T(8,128)(2,1)S(1)} %get-tuple-element.27.refs_0_, bf16[2,128,256]{2,1,0:T(8,128)(2,1)S(1)} %get-tuple-element.28.refs_1_.refs_4_, bf16[27,256,256]{2,1,0:T(8,128)(2,1)S(1)} %get-tuple-element.29.refs_2_.refs_6_), custom_call_target="tpu_custom_call" | custom-call | flops 905969664 | bytes 3538944 | tf_op jit(solution)/shard_map/pallas_call | solution.py:212
  8.2 1.3 %collective-permute-start = (bf16[2,128,256]{2,1,0:T(8,128)(2,1)S(1)}, bf16[2,128,256]{2,1,0:T(8,128)(2,1)S(1)}, u32[]{:S(2)}, u32[]{:S(2)}) collective-permute-start(bf16[2,128,256]{2,1,0:T(8,128)(2,1)S(1)} %shard_map.69.refs_5_), channel_id=1, source_target_pairs={{32,0},{64,32},{96,64},{128,96},{160,128},{192,160},{224,192},{33,... | collective-permute-start | bytes 393224 | tf_op jit(solution)/shard_map/ppermute | solution.py:46
  9.5 1.3 %collective-permute-start.1 = (bf16[2,128,256]{2,1,0:T(8,128)(2,1)S(1)}, bf16[2,128,256]{2,1,0:T(8,128)(2,1)S(1)}, u32[]{:S(2)}, u32[]{:S(2)}) collective-permute-start(bf16[2,128,256]{2,1,0:T(8,128)(2,1)S(1)} %get-tuple-element.28.refs_1_.refs_4_), channel_id=1, source_target_pairs={{32,0},{64,32},{96,64},{128,96},{160,128},{192,160},{224,192},{33,... | collective-permute-start | bytes 393224 | tf_op jit(solution)/shard_map/ppermute | solution.py:46
  10.8 3.3 %collective-permute-start.6 = (bf16[2,384,128]{2,1,0:T(8,128)(2,1)S(1)}, bf16[2,384,128]{2,1,0:T(8,128)(2,1)S(1)}, u32[]{:S(2)}, u32[]{:S(2)}) collective-permute-start(bf16[2,384,128]{2,1,0:T(8,128)(2,1)S(1)} %get-tuple-element.38.give.refs_1_), channel_id=1, source_target_pairs={{0,1},{1,0},{2,3},{3,2},{4,5},{5,4},{6,7},{7,6},{8,9},{9,8},{10,11... | collective-permute-start | bytes 589832 | tf_op jit(solution)/shard_map/ppermute | solution.py:41
  14.5 2.5 %collective-permute-done.1.refs_1_ = bf16[2,128,256]{2,1,0:T(8,128)(2,1)S(1)} collective-permute-done((bf16[2,128,256]{2,1,0:T(8,128)(2,1)S(1)}, bf16[2,128,256]{2,1,0:T(8,128)(2,1)S(1)}, u32[]{:S(2)}, u32[]{:S(2)}) %collective-permute-start.1) | collective-permute-done | bytes 131104 | tf_op jit(solution)/shard_map/ppermute | solution.py:46
  16.9 2.2 %shard_map.70 = (bf16[2,128,256]{2,1,0:T(8,128)(2,1)S(1)}, bf16[2,384,128]{2,1,0:T(8,128)(2,1)S(1)}, bf16[2,128,128]{2,1,0:T(8,128)(2,1)S(1)}) custom-call(s32[8]{0:T(128)S(1)} %compare_select_fusion.4.place, bf16[2,128,256]{2,1,0:T(8,128)(2,1)S(1)} %collective-permute-done.refs_0_, bf16[2,128,256]{2,1,0:T(8,128)(2,1)S(1)} %collective-permute-done.1.refs_1_, ...), custom_call_target="tpu_custom_call" | custom-call | flops 905969664 | bytes 3538944 | tf_op jit(solution)/shard_map/pallas_call | solution.py:212
  19.1 3.3 %collective-permute-start.2 = (bf16[2,384,128]{2,1,0:T(8,128)(2,1)S(1)}, bf16[2,384,128]{2,1,0:T(8,128)(2,1)S(1)}, u32[]{:S(2)}, u32[]{:S(2)}) collective-permute-start(bf16[2,384,128]{2,1,0:T(8,128)(2,1)S(1)} %get-tuple-element.33.give.refs_1_), channel_id=1, source_target_pairs={{0,1},{1,0},{2,3},{3,2},{4,5},{5,4},{6,7},{7,6},{8,9},{9,8},{10,11... | collective-permute-start | bytes 589832 | tf_op jit(solution)/shard_map/ppermute | solution.py:41
  23.3 2.6 %collective-permute-start.8 = (bf16[2,2,192,128]{3,2,1,0:T(8,128)(2,1)S(1)}, bf16[2,2,192,128]{3,2,1,0:T(8,128)(2,1)S(1)}, u32[]{:S(2)}, u32[]{:S(2)}) collective-permute-start(bf16[2,2,192,128]{3,2,1,0:T(8,128)(2,1)S(1)} %get-tuple-element.40), channel_id=1, source_target_pairs={{0,4},{1,5},{2,6},{3,7},{4,0},{5,1},{6,2},{7,3},{8,12},{9,13},{10,... | collective-permute-start | bytes 589832 | tf_op jit(solution)/shard_map/ppermute | solution.py:41
  28.4 1.9 %collective-permute-done.7.refs_3_ = bf16[2,2,192,128]{3,2,1,0:T(8,128)(2,1)S(1)} collective-permute-done((bf16[2,2,192,128]{3,2,1,0:T(8,128)(2,1)S(1)}, bf16[2,2,192,128]{3,2,1,0:T(8,128)(2,1)S(1)}, u32[]{:S(2)}, u32[]{:S(2)}) %collective-permute-start.7) | collective-permute-done | bytes 196640 | tf_op jit(solution)/shard_map/ppermute | solution.py:41
  31.2 4.0 %collective-permute-done.8.refs_4_ = bf16[2,2,192,128]{3,2,1,0:T(8,128)(2,1)S(1)} collective-permute-done((bf16[2,2,192,128]{3,2,1,0:T(8,128)(2,1)S(1)}, bf16[2,2,192,128]{3,2,1,0:T(8,128)(2,1)S(1)}, u32[]{:S(2)}, u32[]{:S(2)}) %collective-permute-start.8) | collective-permute-done | bytes 196640 | tf_op jit(solution)/shard_map/ppermute | solution.py:41
  35.2 2.2 %shard_map.74.refs_6_ = f32[2,3,576,128]{3,2,1,0:T(8,128)S(1)} custom-call(bf16[2,128,128]{2,1,0:T(8,128)(2,1)S(1)} %get-tuple-element.37.mine.refs_0_, bf16[2,384,128]{2,1,0:T(8,128)(2,1)S(1)} %get-tuple-element.38.give.refs_1_, bf16[2,384,128]{2,1,0:T(8,128)(2,1)S(1)} %collective-permute-done.6.got.refs_2_, ...), custom_call_target="tpu_custom_call" | custom-call | flops 905969664 | bytes 4194304 | tf_op jit(solution)/shard_map/pallas_call | solution.py:307
  37.4 1.6 %collective-permute-done.3.refs_3_ = bf16[2,2,192,128]{3,2,1,0:T(8,128)(2,1)S(1)} collective-permute-done((bf16[2,2,192,128]{3,2,1,0:T(8,128)(2,1)S(1)}, bf16[2,2,192,128]{3,2,1,0:T(8,128)(2,1)S(1)}, u32[]{:S(2)}, u32[]{:S(2)}) %collective-permute-start.3) | collective-permute-done | bytes 196640 | tf_op jit(solution)/shard_map/ppermute | solution.py:41
  38.9 4.7 %collective-permute-done.4.refs_4_ = bf16[2,2,192,128]{3,2,1,0:T(8,128)(2,1)S(1)} collective-permute-done((bf16[2,2,192,128]{3,2,1,0:T(8,128)(2,1)S(1)}, bf16[2,2,192,128]{3,2,1,0:T(8,128)(2,1)S(1)}, u32[]{:S(2)}, u32[]{:S(2)}) %collective-permute-start.4) | collective-permute-done | bytes 196640 | tf_op jit(solution)/shard_map/ppermute | solution.py:41
  44.8 6.1 %collective-permute-start.12 = (bf16[2,27,16,128]{3,2,1,0:T(8,128)(2,1)S(1)}, bf16[2,27,16,128]{3,2,1,0:T(8,128)(2,1)S(1)}, u32[]{:S(2)}, u32[]{:S(2)}) collective-permute-start(bf16[2,27,16,128]{3,2,1,0:T(8,128)(2,1)S(1)} %get-tuple-element.47), channel_id=1, source_target_pairs={{0,24},{1,25},{2,26},{3,27},{4,28},{5,29},{6,30},{7,31},{8,16},{9,... | collective-permute-start | bytes 663560 | tf_op jit(solution)/shard_map/ppermute | solution.py:41
  52.1 1.3 %collective-permute-start.10 = (bf16[2,27,16,128]{3,2,1,0:T(8,128)(2,1)S(1)}, bf16[2,27,16,128]{3,2,1,0:T(8,128)(2,1)S(1)}, u32[]{:S(2)}, u32[]{:S(2)}) collective-permute-start(bf16[2,27,16,128]{3,2,1,0:T(8,128)(2,1)S(1)} %get-tuple-element.43), channel_id=1, source_target_pairs={{0,8},{1,9},{2,10},{3,11},{4,12},{5,13},{6,14},{7,15},{8,0},{9,1},... | collective-permute-start | bytes 663560 | tf_op jit(solution)/shard_map/ppermute | solution.py:41
  53.4 2.5 %collective-permute-done.12.got = bf16[2,27,16,128]{3,2,1,0:T(8,128)(2,1)S(1)} collective-permute-done((bf16[2,27,16,128]{3,2,1,0:T(8,128)(2,1)S(1)}, bf16[2,27,16,128]{3,2,1,0:T(8,128)(2,1)S(1)}, u32[]{:S(2)}, u32[]{:S(2)}) %collective-permute-start.12) | collective-permute-done | bytes 221216 | tf_op jit(solution)/shard_map/ppermute | solution.py:41
  56.0 2.2 %collective-permute-start.13 = (bf16[27,16,128]{2,1,0:T(8,128)(2,1)S(1)}, bf16[27,16,128]{2,1,0:T(8,128)(2,1)S(1)}, u32[]{:S(2)}, u32[]{:S(2)}) collective-permute-start(bf16[27,16,128]{2,1,0:T(8,128)(2,1)S(1)} %get-tuple-element.49), channel_id=1, source_target_pairs={{0,8},{1,9},{2,10},{3,11},{4,12},{5,13},{6,14},{7,15},{8,0},{9,1},... | collective-permute-start | bytes 331784 | tf_op jit(solution)/shard_map/ppermute | solution.py:41
  58.2 5.6 %collective-permute-done.10.got = bf16[2,27,16,128]{3,2,1,0:T(8,128)(2,1)S(1)} collective-permute-done((bf16[2,27,16,128]{3,2,1,0:T(8,128)(2,1)S(1)}, bf16[2,27,16,128]{3,2,1,0:T(8,128)(2,1)S(1)}, u32[]{:S(2)}, u32[]{:S(2)}) %collective-permute-start.10) | collective-permute-done | bytes 221216 | tf_op jit(solution)/shard_map/ppermute | solution.py:41
  63.9 2.2 %collective-permute-done.13.last_g = bf16[27,16,128]{2,1,0:T(8,128)(2,1)S(1)} collective-permute-done((bf16[27,16,128]{2,1,0:T(8,128)(2,1)S(1)}, bf16[27,16,128]{2,1,0:T(8,128)(2,1)S(1)}, u32[]{:S(2)}, u32[]{:S(2)}) %collective-permute-start.13) | collective-permute-done | bytes 110624 | tf_op jit(solution)/shard_map/ppermute | solution.py:41
  66.1 5.4 %collective-permute-done.11.last_f = bf16[27,16,128]{2,1,0:T(8,128)(2,1)S(1)} collective-permute-done((bf16[27,16,128]{2,1,0:T(8,128)(2,1)S(1)}, bf16[27,16,128]{2,1,0:T(8,128)(2,1)S(1)}, u32[]{:S(2)}, u32[]{:S(2)}) %collective-permute-start.11) | collective-permute-done | bytes 110624 | tf_op jit(solution)/shard_map/ppermute | solution.py:41
  72.2 4.8 %collective-permute-start.14 = (bf16[2,27,8,128]{3,2,1,0:T(8,128)(2,1)S(1)}, bf16[2,27,8,128]{3,2,1,0:T(8,128)(2,1)S(1)}, u32[]{:S(2)}, u32[]{:S(2)}) collective-permute-start(bf16[2,27,8,128]{3,2,1,0:T(8,128)(2,1)S(1)} %get-tuple-element.51), channel_id=1, source_target_pairs={{0,1},{1,0},{2,3},{3,2},{4,5},{5,4},{6,7},{7,6},{8,9},{9,8},{10,11... | collective-permute-start | bytes 331784 | tf_op jit(solution)/shard_map/ppermute | solution.py:41
  77.0 2.9 %shard_map.71 = bf16[2,4,128,256]{3,2,1,0:T(8,128)(2,1)} custom-call(s32[8]{0:T(128)S(1)} %compare_select_fusion.4.place, bf16[2,128,256]{2,1,0:T(8,128)(2,1)S(1)} %collective-permute-done.refs_0_, bf16[2,128,256]{2,1,0:T(8,128)(2,1)S(1)} %collective-permute-done.1.refs_1_, bf16[2,128,256]{2,1,0:T(8,128)(2,1)S(1)} %get-tuple-element.31.refs_2_, ...), custom_call_target="tpu_custom_call" | custom-call | flops 905969664 | bytes 3538944 | tf_op jit(solution)/shard_map/pallas_call | solution.py:212
  79.9 1.4 %shard_map.80 = f32[2,27,8,256]{3,2,1,0:T(8,128)} custom-call(s32[8]{0:T(128)S(1)} %compare_select_fusion.4.place, f32[2,27,8,128]{3,2,1,0:T(8,128)S(1)} %get-tuple-element.50.mine, bf16[2,27,8,128]{3,2,1,0:T(8,128)(2,1)S(1)} %collective-permute-done.14.got, f32[2,27,8,256]{3,2,1,0:T(8,128)S(1)} %bitcast.9), custom_call_target="tpu_custom_call" | custom-call | bytes 1048576 | tf_op jit(solution)/shard_map/pallas_call | solution.py:319
  (24 shorter events, 7.9 us)
Async XLA Ops:
  6.0 10.9 %copy-start = (bf16[4,4,128,256]{3,2,1,0:T(8,128)(2,1)S(1)}, bf16[4,4,128,256]{3,2,1,0:T(8,128)(2,1)}, u32[]{:S(2)}) copy-start(bf16[4,4,128,256]{3,2,1,0:T(8,128)(2,1)} %refs_3_.1) | copy-start | bytes 3145732
  8.2 6.3 %collective-permute-start = (bf16[2,128,256]{2,1,0:T(8,128)(2,1)S(1)}, bf16[2,128,256]{2,1,0:T(8,128)(2,1)S(1)}, u32[]{:S(2)}, u32[]{:S(2)}) collective-permute-start(bf16[2,128,256]{2,1,0:T(8,128)(2,1)S(1)} %shard_map.69.refs_5_), channel_id=1, source_target_pairs={{32,0},{64,32},{96,64},{128,96},{160,128},{192,160},{224,192},{33,... | collective-permute-start | bytes 393224 | tf_op jit(solution)/shard_map/ppermute | solution.py:46
  9.5 7.5 %collective-permute-start.1 = (bf16[2,128,256]{2,1,0:T(8,128)(2,1)S(1)}, bf16[2,128,256]{2,1,0:T(8,128)(2,1)S(1)}, u32[]{:S(2)}, u32[]{:S(2)}) collective-permute-start(bf16[2,128,256]{2,1,0:T(8,128)(2,1)S(1)} %get-tuple-element.28.refs_1_.refs_4_), channel_id=1, source_target_pairs={{32,0},{64,32},{96,64},{128,96},{160,128},{192,160},{224,192},{33,... | collective-permute-start | bytes 393224 | tf_op jit(solution)/shard_map/ppermute | solution.py:46
  10.8 11.7 %collective-permute-start.6 = (bf16[2,384,128]{2,1,0:T(8,128)(2,1)S(1)}, bf16[2,384,128]{2,1,0:T(8,128)(2,1)S(1)}, u32[]{:S(2)}, u32[]{:S(2)}) collective-permute-start(bf16[2,384,128]{2,1,0:T(8,128)(2,1)S(1)} %get-tuple-element.38.give.refs_1_), channel_id=1, source_target_pairs={{0,1},{1,0},{2,3},{3,2},{4,5},{5,4},{6,7},{7,6},{8,9},{9,8},{10,11... | collective-permute-start | bytes 589832 | tf_op jit(solution)/shard_map/ppermute | solution.py:41
  19.1 7.9 %collective-permute-start.2 = (bf16[2,384,128]{2,1,0:T(8,128)(2,1)S(1)}, bf16[2,384,128]{2,1,0:T(8,128)(2,1)S(1)}, u32[]{:S(2)}, u32[]{:S(2)}) collective-permute-start(bf16[2,384,128]{2,1,0:T(8,128)(2,1)S(1)} %get-tuple-element.33.give.refs_1_), channel_id=1, source_target_pairs={{0,1},{1,0},{2,3},{3,2},{4,5},{5,4},{6,7},{7,6},{8,9},{9,8},{10,11... | collective-permute-start | bytes 589832 | tf_op jit(solution)/shard_map/ppermute | solution.py:41
  22.5 7.7 %collective-permute-start.7 = (bf16[2,2,192,128]{3,2,1,0:T(8,128)(2,1)S(1)}, bf16[2,2,192,128]{3,2,1,0:T(8,128)(2,1)S(1)}, u32[]{:S(2)}, u32[]{:S(2)}) collective-permute-start(bf16[2,2,192,128]{3,2,1,0:T(8,128)(2,1)S(1)} %get-tuple-element.39), channel_id=1, source_target_pairs={{0,2},{1,3},{2,4},{3,5},{4,6},{5,7},{6,0},{7,1},{8,10},{9,11},{10,... | collective-permute-start | bytes 589832 | tf_op jit(solution)/shard_map/ppermute | solution.py:41
  23.3 11.9 %collective-permute-start.8 = (bf16[2,2,192,128]{3,2,1,0:T(8,128)(2,1)S(1)}, bf16[2,2,192,128]{3,2,1,0:T(8,128)(2,1)S(1)}, u32[]{:S(2)}, u32[]{:S(2)}) collective-permute-start(bf16[2,2,192,128]{3,2,1,0:T(8,128)(2,1)S(1)} %get-tuple-element.40), channel_id=1, source_target_pairs={{0,4},{1,5},{2,6},{3,7},{4,0},{5,1},{6,2},{7,3},{8,12},{9,13},{10,... | collective-permute-start | bytes 589832 | tf_op jit(solution)/shard_map/ppermute | solution.py:41
  26.0 9.2 %collective-permute-start.9 = (bf16[2,2,192,128]{3,2,1,0:T(8,128)(2,1)S(1)}, bf16[2,2,192,128]{3,2,1,0:T(8,128)(2,1)S(1)}, u32[]{:S(2)}, u32[]{:S(2)}) collective-permute-start(bf16[2,2,192,128]{3,2,1,0:T(8,128)(2,1)S(1)} %get-tuple-element.41), channel_id=1, source_target_pairs={{0,6},{1,7},{2,0},{3,1},{4,2},{5,3},{6,4},{7,5},{8,14},{9,15},{10,... | collective-permute-start | bytes 589832 | tf_op jit(solution)/shard_map/ppermute | solution.py:41
  27.1 11.8 %collective-permute-start.3 = (bf16[2,2,192,128]{3,2,1,0:T(8,128)(2,1)S(1)}, bf16[2,2,192,128]{3,2,1,0:T(8,128)(2,1)S(1)}, u32[]{:S(2)}, u32[]{:S(2)}) collective-permute-start(bf16[2,2,192,128]{3,2,1,0:T(8,128)(2,1)S(1)} %get-tuple-element.34), channel_id=1, source_target_pairs={{0,2},{1,3},{2,4},{3,5},{4,6},{5,7},{6,0},{7,1},{8,10},{9,11},{10,... | collective-permute-start | bytes 589832 | tf_op jit(solution)/shard_map/ppermute | solution.py:41
  27.6 16.0 %collective-permute-start.4 = (bf16[2,2,192,128]{3,2,1,0:T(8,128)(2,1)S(1)}, bf16[2,2,192,128]{3,2,1,0:T(8,128)(2,1)S(1)}, u32[]{:S(2)}, u32[]{:S(2)}) collective-permute-start(bf16[2,2,192,128]{3,2,1,0:T(8,128)(2,1)S(1)} %get-tuple-element.35), channel_id=1, source_target_pairs={{0,4},{1,5},{2,6},{3,7},{4,0},{5,1},{6,2},{7,3},{8,12},{9,13},{10,... | collective-permute-start | bytes 589832 | tf_op jit(solution)/shard_map/ppermute | solution.py:41
  30.2 13.4 %collective-permute-start.5 = (bf16[2,2,192,128]{3,2,1,0:T(8,128)(2,1)S(1)}, bf16[2,2,192,128]{3,2,1,0:T(8,128)(2,1)S(1)}, u32[]{:S(2)}, u32[]{:S(2)}) collective-permute-start(bf16[2,2,192,128]{3,2,1,0:T(8,128)(2,1)S(1)} %get-tuple-element.36), channel_id=1, source_target_pairs={{0,6},{1,7},{2,0},{3,1},{4,2},{5,3},{6,4},{7,5},{8,14},{9,15},{10,... | collective-permute-start | bytes 589832 | tf_op jit(solution)/shard_map/ppermute | solution.py:41
  44.8 11.1 %collective-permute-start.12 = (bf16[2,27,16,128]{3,2,1,0:T(8,128)(2,1)S(1)}, bf16[2,27,16,128]{3,2,1,0:T(8,128)(2,1)S(1)}, u32[]{:S(2)}, u32[]{:S(2)}) collective-permute-start(bf16[2,27,16,128]{3,2,1,0:T(8,128)(2,1)S(1)} %get-tuple-element.47), channel_id=1, source_target_pairs={{0,24},{1,25},{2,26},{3,27},{4,28},{5,29},{6,30},{7,31},{8,16},{9,... | collective-permute-start | bytes 663560 | tf_op jit(solution)/shard_map/ppermute | solution.py:41
  52.1 11.7 %collective-permute-start.10 = (bf16[2,27,16,128]{3,2,1,0:T(8,128)(2,1)S(1)}, bf16[2,27,16,128]{3,2,1,0:T(8,128)(2,1)S(1)}, u32[]{:S(2)}, u32[]{:S(2)}) collective-permute-start(bf16[2,27,16,128]{3,2,1,0:T(8,128)(2,1)S(1)} %get-tuple-element.43), channel_id=1, source_target_pairs={{0,8},{1,9},{2,10},{3,11},{4,12},{5,13},{6,14},{7,15},{8,0},{9,1},... | collective-permute-start | bytes 663560 | tf_op jit(solution)/shard_map/ppermute | solution.py:41
  55.9 24.0 %copy-start.1 = (f32[1,2,27,8,256]{4,3,2,1,0:T(8,128)S(1)}, f32[1,2,27,8,256]{4,3,2,1,0:T(8,128)}, u32[]{:S(2)}) copy-start(f32[1,2,27,8,256]{4,3,2,1,0:T(8,128)} %param.9) | copy-start | bytes 1327108
  56.0 10.2 %collective-permute-start.13 = (bf16[27,16,128]{2,1,0:T(8,128)(2,1)S(1)}, bf16[27,16,128]{2,1,0:T(8,128)(2,1)S(1)}, u32[]{:S(2)}, u32[]{:S(2)}) collective-permute-start(bf16[27,16,128]{2,1,0:T(8,128)(2,1)S(1)} %get-tuple-element.49), channel_id=1, source_target_pairs={{0,8},{1,9},{2,10},{3,11},{4,12},{5,13},{6,14},{7,15},{8,0},{9,1},... | collective-permute-start | bytes 331784 | tf_op jit(solution)/shard_map/ppermute | solution.py:41
  63.8 7.7 %collective-permute-start.11 = (bf16[27,16,128]{2,1,0:T(8,128)(2,1)S(1)}, bf16[27,16,128]{2,1,0:T(8,128)(2,1)S(1)}, u32[]{:S(2)}, u32[]{:S(2)}) collective-permute-start(bf16[27,16,128]{2,1,0:T(8,128)(2,1)S(1)} %get-tuple-element.45), channel_id=1, source_target_pairs={{0,24},{1,25},{2,26},{3,27},{4,28},{5,29},{6,30},{7,31},{8,16},{9,... | collective-permute-start | bytes 331784 | tf_op jit(solution)/shard_map/ppermute | solution.py:41
  72.2 7.8 %collective-permute-start.14 = (bf16[2,27,8,128]{3,2,1,0:T(8,128)(2,1)S(1)}, bf16[2,27,8,128]{3,2,1,0:T(8,128)(2,1)S(1)}, u32[]{:S(2)}, u32[]{:S(2)}) collective-permute-start(bf16[2,27,8,128]{3,2,1,0:T(8,128)(2,1)S(1)} %get-tuple-element.51), channel_id=1, source_target_pairs={{0,1},{1,0},{2,3},{3,2},{4,5},{5,4},{6,7},{7,6},{8,9},{9,8},{10,11... | collective-permute-start | bytes 331784 | tf_op jit(solution)/shard_map/ppermute | solution.py:41
